TPU v7x, 512 devices: a whole 4x8x8 slice. The times are simulated.
512 devices in a mesh: dp: 64 (over x, y, z_hi), head: 8 (over z_lo, core).
Axes of the slice: x: 4, y: 8, z: 8 (z_hi: 2, z_lo: 4; z = z_hi * 4 + z_lo), core: 2. Of those that a mesh axis runs over, the one named last changes fastest.
Arguments:
- tokens: bfloat16 [16384, 8192], P('dp', 'head'), may hold values from -6 to 6
- key_weight: bfloat16 [8192, 1024], P('dp', 'head'), may hold values from -0.0625 to 0.0625
- queries: bfloat16 [16384, 8192], P('dp', 'head'), may hold values from -51 to 51
- values: bfloat16 [16384, 1024], P('dp', 'head'), may hold values from -6 to 6
- out_grad: bfloat16 [16384, 8192], P('dp', 'head'), may hold values from -6 to 6
Outputs:
- query_grad: bfloat16 [16384, 8192], P('dp', 'head')
- value_grad: bfloat16 [16384, 1024], P('dp', 'head')
- weight_grad: float32 [8192, 1024], P('dp', 'head')
All inputs are finite; a program needn't handle non-finite values.
Results may differ from a plain program's by a relative error of at most 0.022.
The roundings to bfloat16 on the way count: a program that leaves them out, or rounds other values in their place, can miss the bound.
Values may be sent and summed in bfloat16 or wider, within the bound.
No kernel may reach another device: no remote copies, remote signals or barrier semaphores. Data moves between devices by JAX's collectives and lax.ppermute only.
A program may use at most 64 MiB of HBM per device.

v0:
```python
import jax
import jax.numpy as jnp
from jax import lax
from jax.sharding import PartitionSpec as P


def on_device(tokens, key_weight, queries, values, out_grad):
    width = values.shape[1]
    length = tokens.shape[0]
    group = queries.shape[1] // width
    scale = width ** (-0.5)
    gathered = lax.all_gather(tokens, "head", axis=1, tiled=True)
    columns = gathered
    keys = jnp.dot(
        columns,
        lax.all_gather(key_weight, "dp", axis=0, tiled=True),
        preferred_element_type=jnp.float32,
    ).astype(jnp.bfloat16)
    query_heads = queries.reshape(length, group, width)
    grad_heads = out_grad.reshape(length, group, width)
    scores = (
        jnp.einsum("qgd,kd->gqk", query_heads, keys, preferred_element_type=jnp.float32) * scale
    )
    rows = lax.broadcasted_iota(jnp.int32, (length, length), 0)
    cols = lax.broadcasted_iota(jnp.int32, (length, length), 1)
    keep = rows >= cols
    scores = jnp.where(keep, scores, jnp.float32(-1e30))
    top = jnp.max(scores, axis=-1, keepdims=True)
    expo = jnp.where(keep, jnp.exp(scores - top), jnp.float32(0.0))
    probs = expo / jnp.sum(expo, axis=-1, keepdims=True)
    weights = probs.astype(jnp.bfloat16)
    attended = jnp.einsum(
        "gqk,kd->qgd", weights, values, preferred_element_type=jnp.float32
    ).astype(jnp.bfloat16)
    dprobs = jnp.einsum("qgd,kd->gqk", grad_heads, values, preferred_element_type=jnp.float32)
    delta = jnp.transpose(
        jnp.sum(grad_heads.astype(jnp.float32) * attended.astype(jnp.float32), axis=-1), (1, 0)
    )
    dscores = (probs * (dprobs - delta[..., None])).astype(jnp.bfloat16)
    query_grad = (
        jnp.einsum("gqk,kd->qgd", dscores, keys, preferred_element_type=jnp.float32) * scale
    ).astype(jnp.bfloat16)
    key_grad = (
        jnp.einsum("gqk,qgd->kd", dscores, query_heads, preferred_element_type=jnp.float32) * scale
    ).astype(jnp.bfloat16)
    value_grad = jnp.einsum(
        "gqk,qgd->kd", weights, grad_heads, preferred_element_type=jnp.float32
    ).astype(jnp.bfloat16)
    columns = gathered
    weight_grad = lax.psum_scatter(
        lax.dot_general(
            columns, key_grad, (((0,), (0,)), ((), ())), preferred_element_type=jnp.float32
        ),
        "dp",
        scatter_dimension=0,
        tiled=True,
    )
    return (query_grad.reshape(length, group * width), value_grad, weight_grad)


def solution(mesh):
    placed = (P("dp", "head"), P("dp", "head"), P("dp", "head"), P("dp", "head"), P("dp", "head"))
    return jax.shard_map(
        on_device,
        mesh=mesh,
        in_specs=placed,
        out_specs=(P("dp", "head"), P("dp", "head"), P("dp", "head")),
        check_vma=False,
    )
```

profile of v0, /device:TPU:64, one launch (start us, length us, event | category | flops | bytes accessed | tf_op | source)
XLA Modules:
  0.0 685.2 jit_solution(2538484777238833299)
XLA Ops:
  7.2 0.0 copy-start
  7.2 0.0 all-gather.5.cloned.1.call-start
  7.2 0.7 all-gather.5.cloned.1.call-update
  7.9 0.0 all-gather.3.cloned.1.call-start
  8.0 0.7 all-gather.3.cloned.1.call-update
  8.7 0.0 reduce-scatter.2.cloned.1.call-start
  8.7 1.2 copy.9
  10.0 144.5 %all-gather.5.cloned.1.call-done = bf16[8192,128]{1,0:T(8,128)(2,1)} async-done(((bf16[128,128]{1,0:T(8,128)(2,1)}), bf16[8192,128]{1,0:T(8,128)(2,1)}) %all-gather.5.cloned.1.call-update) | async-done | bytes 2097168 | tf_op jit(solution)/shard_map/all_gather | solution.py:16
  154.5 48.9 %all-gather.3.cloned.1.call-done = bf16[256,8192]{1,0:T(8,128)(2,1)} async-done(((bf16[256,1024]{1,0:T(8,128)(2,1)}), bf16[256,8192]{1,0:T(8,128)(2,1)}) %all-gather.3.cloned.1.call-update) | async-done | bytes 4194320 | tf_op jit(solution)/shard_map/all_gather | solution.py:12
  203.5 4.1 fusion.12
  207.6 0.0 copy-done
  207.6 2.3 fusion.36
  209.8 0.0 copy-start.2
  209.8 0.0 copy-start.1
  209.8 1.9 fusion.16
  211.8 0.0 copy-done.2
  211.8 0.4 fusion.8
  212.2 0.0 copy-done.1
  212.2 0.4 fusion.2
  212.6 5.3 convolution_bitcast_fusion
  217.9 0.0 reduce-scatter.2.cloned.1.call-update
  217.9 1.1 fusion.7
  219.0 2.0 copy.16
  221.1 1.1 fusion.10
  222.1 454.9 %reduce-scatter.2.cloned.1.call-done = f32[128,128]{0,1:T(8,128)} async-done(((f32[8192,128]{0,1:T(8,128)}), f32[128,128]{0,1:T(8,128)}) %reduce-scatter.2.cloned.1.call-update) | async-done | bytes 65552 | tf_op jit(solution)/shard_map/reduce_scatter | solution.py:50
  677.1 1.6 copy.17
  (1 shorter events, 0.0 us)
Async XLA Ops:
  7.2 200.4 %copy-start = (bf16[256,1024]{1,0:T(8,128)(2,1)S(1)}, bf16[256,1024]{1,0:T(8,128)(2,1)}, u32[]{:S(2)}) copy-start(bf16[256,1024]{1,0:T(8,128)(2,1)} %param.7) | copy-start | bytes 1572868
  7.2 147.4 %all-gather.5.cloned.1.call-start = ((), (), s32[]{:S(2)}) async-start(), calls=%async_computation.2 | async-start | bytes 2129920 | tf_op jit(solution)/shard_map/all_gather | solution.py:16
  7.9 195.5 %all-gather.3.cloned.1.call-start = ((), (), s32[]{:S(2)}) async-start(), calls=%async_computation.1 | async-start | bytes 4718592 | tf_op jit(solution)/shard_map/all_gather | solution.py:12
  8.7 668.4 %reduce-scatter.2.cloned.1.call-start = ((), (), s32[]{:S(2)}) async-start(), calls=%async_computation.3 | async-start | bytes 4259840 | tf_op jit(solution)/shard_map/reduce_scatter | solution.py:50
  209.8 1.9 copy-start.2
  209.8 2.3 copy-start.1
Sparse Core Ops, SparseCore 0:
  12.5 141.9 all-gather.4
  156.6 46.7 all-gather.2
  218.1 458.9 reduce-scatter.1
where the time goes:
time: 685 us
  waiting for transfers between devices  650 us (95%)
  matrix products  14.7 us (2%)
  between operations  13.8 us (2%)
    reduce_scatter x1, waiting for transfers between devices, on_device(): lax.psum_scatter(lax.dot_general(columns, key_grad, (((0,), (0,)), ((), (...  455 us
    all_gather x1, waiting for transfers between devices, on_device(): lax.all_gather(key_weight, 'dp', axis=0, tiled=True)  145 us
    all_gather x1, waiting for transfers between devices, on_device(): gathered = lax.all_gather(tokens, 'head', axis=1, tiled=True)  48.9 us
  transfers between devices with their start and end apart: 3, of which 3 were waited for; matrix products, arithmetic and copies ran while one was open for 1% of the time, Pallas kernels for 0%

commit v1 on v0

--- a/solution.py
+++ b/solution.py
@@ -3,19 +3,51 @@
 from jax import lax
 from jax.sharding import PartitionSpec as P
 
+X, Y, ZH, ZL, C = 4, 8, 2, 4, 2
 
-def on_device(tokens, key_weight, queries, values, out_grad):
+
+def dp_of(x, y, zh):
+    return ((x % X) * Y + y) * ZH + zh
+
+
+def place(x, y, zh, zl, c):
+    return dp_of(x, y, zh) * ZL * C + (zl % ZL) * C + c
+
+
+CHIPS = [
+    (x, y, zh, zl, c)
+    for x in range(X)
+    for y in range(Y)
+    for zh in range(ZH)
+    for zl in range(ZL)
+    for c in range(C)
+]
+ALONG_X = [[dp_of(x, y, zh) for x in range(X)] for y in range(Y) for zh in range(ZH)]
+ALONG_YZ = [[dp_of(x, y, zh) for y in range(Y) for zh in range(ZH)] for x in range(X)]
+CORES = [(h, h ^ 1) for h in range(ZL * C)]
+
+
+def turned(j):
+    return [(place(x, y, zh, zl, c), place(zl, y, zh, x + j, c)) for x, y, zh, zl, c in CHIPS]
+
+
+def spread(block, groups):
+    n = len(groups[0])
+    many = jnp.broadcast_to(block[None], (n,) + block.shape)
+    return lax.all_to_all(many, "dp", 0, 0, tiled=True, axis_index_groups=groups)
+
+
+def reorder(parts, zl):
+    back = parts[::-1]
+    twice = jnp.concatenate([back, back], axis=0)
+    return lax.dynamic_slice_in_dim(twice, X - 1 - zl, X, axis=0)
+
+
+def attention(queries, keys, values, out_grad):
     width = values.shape[1]
-    length = tokens.shape[0]
+    length = queries.shape[0]
     group = queries.shape[1] // width
     scale = width ** (-0.5)
-    gathered = lax.all_gather(tokens, "head", axis=1, tiled=True)
-    columns = gathered
-    keys = jnp.dot(
-        columns,
-        lax.all_gather(key_weight, "dp", axis=0, tiled=True),
-        preferred_element_type=jnp.float32,
-    ).astype(jnp.bfloat16)
     query_heads = queries.reshape(length, group, width)
     grad_heads = out_grad.reshape(length, group, width)
     scores = (
@@ -46,16 +78,49 @@
     value_grad = jnp.einsum(
         "gqk,qgd->kd", weights, grad_heads, preferred_element_type=jnp.float32
     ).astype(jnp.bfloat16)
-    columns = gathered
-    weight_grad = lax.psum_scatter(
-        lax.dot_general(
-            columns, key_grad, (((0,), (0,)), ((), ())), preferred_element_type=jnp.float32
-        ),
-        "dp",
-        scatter_dimension=0,
-        tiled=True,
+    return query_grad.reshape(length, group * width), key_grad, value_grad
+
+
+def on_device(tokens, key_weight, queries, values, out_grad):
+    f32 = jnp.float32
+    length, feats = tokens.shape
+    head = lax.axis_index("head")
+    zl, c = head // C, head % C
+    mine = [lax.ppermute(tokens, ("dp", "head"), turned(j)) for j in range(X)]
+    weight = spread(key_weight, ALONG_YZ).reshape(C * feats, -1)
+    width = weight.shape[1]
+    theirs = [lax.ppermute(block, "head", CORES) for block in mine]
+    near = lax.dynamic_slice_in_dim(weight, c * feats, feats, axis=0)
+    far = lax.dynamic_slice_in_dim(weight, (1 - c) * feats, feats, axis=0)
+    partial = jnp.stack(
+        [
+            jnp.dot(a, near, preferred_element_type=f32) + jnp.dot(b, far, preferred_element_type=f32)
+            for a, b in zip(mine, theirs)
+        ]
     )
-    return (query_grad.reshape(length, group * width), value_grad, weight_grad)
+    partial = lax.all_to_all(
+        reorder(partial, zl), "dp", 0, 0, tiled=True, axis_index_groups=ALONG_X
+    )
+    keys = jnp.sum(partial, axis=0).astype(jnp.bfloat16)
+    query_grad, key_grad, value_grad = attention(queries, keys, values, out_grad)
+    grads = reorder(spread(key_grad, ALONG_X).reshape(X, length, width), zl)
+
+    def contracted(blocks):
+        return sum(
+            lax.dot_general(
+                a, grads[j], (((0,), (0,)), ((), ())), preferred_element_type=f32
+            )
+            for j, a in enumerate(blocks)
+        )
+
+    own, other = contracted(mine), contracted(theirs)
+    rows = jnp.concatenate([own, other, own], axis=0).astype(jnp.bfloat16)
+    rows = lax.dynamic_slice_in_dim(rows, c * feats, C * feats, axis=0)
+    rows = lax.all_to_all(
+        rows.reshape(Y * ZH, -1, width), "dp", 0, 0, tiled=True, axis_index_groups=ALONG_YZ
+    )
+    weight_grad = jnp.sum(rows.astype(f32), axis=0)
+    return query_grad, value_grad, weight_grad
 
 
 def solution(mesh):

time: 685 us -> 180 us (0.26)
  waiting for transfers between devices: 650 us -> 82.5 us
  starting transfers between devices: 0.11 us -> 64.9 us
  between operations: 13.8 us -> 1.11 us
    reduce_scatter x1 -> x0, waiting for transfers between devices: 455 us -> none  [on_device(): lax.psum_scatter(lax.dot_general(columns, key_grad, (((0,), (0,)), ((), (...]
    all_gather x2 -> x0, waiting for transfers between devices: 193 us -> none  [the longest x1 145 us: on_device(): lax.all_gather(key_weight, 'dp', axis=0, tiled=True)]
    ppermute x0 -> x8, waiting for transfers between devices: none -> 50.8 us  [the longest x4 50.8 us: on_device(): mine = [lax.ppermute(tokens, ('dp', 'head'), turned(j)) for j in range(X)]]
    all_to_all x0 -> x4, starting transfers between devices: none -> 40.4 us  [the longest x2 18.8 us: spread(): lax.all_to_all(many, 'dp', 0, 0, tiled=True, axis_index_groups=groups)]
    all_to_all x0 -> x4, waiting for transfers between devices: none -> 31.7 us  [the longest x1 15.5 us: on_device(): lax.all_to_all(rows.reshape(Y * ZH, -1, width), 'dp', 0, 0, tiled=True, a...]
    ppermute x0 -> x8, starting transfers between devices: none -> 24.5 us  [the longest x4 16.9 us: on_device(): mine = [lax.ppermute(tokens, ('dp', 'head'), turned(j)) for j in range(X)]]
    dot_general x6 -> x21, matrix products: 12.4 us -> 16.8 us  [the longest x8 6.29 us: contracted(): lax.dot_general(a, grads[j], (((0,), (0,)), ((), ())), preferred_element_...]
  transfers between devices with their start and end apart: 3 -> 12, of which waited for: 3 -> 7; matrix products, arithmetic and copies ran while one was open for 1% -> 5% of each run, Pallas kernels for 0% -> 0%
where the time goes in v1:
time: 180 us; the launch traced here: 179 us
  waiting for transfers between devices  82.5 us (46%)
  starting transfers between devices  64.9 us (36%)
  matrix products  19.1 us (11%)
  local copies, waits for them, and re-layouts  7.7 us (4%)
  other arithmetic  3.44 us (2%)
    ppermute x4, waiting for transfers between devices, on_device(): mine = [lax.ppermute(tokens, ('dp', 'head'), turned(j)) for j in range(X)]  50.8 us
    all_to_all x2, starting transfers between devices, spread(): lax.all_to_all(many, 'dp', 0, 0, tiled=True, axis_index_groups=groups)  18.8 us
    ppermute x4, starting transfers between devices, on_device(): mine = [lax.ppermute(tokens, ('dp', 'head'), turned(j)) for j in range(X)]  16.9 us
    all_to_all x1, waiting for transfers between devices, on_device(): lax.all_to_all(rows.reshape(Y * ZH, -1, width), 'dp', 0, 0, tiled=True, a...  15.5 us
    all_to_all x1, starting transfers between devices, on_device(): lax.all_to_all(rows.reshape(Y * ZH, -1, width), 'dp', 0, 0, tiled=True, a...  11.7 us
    all_to_all x1, starting transfers between devices, on_device(): lax.all_to_all(reorder(partial, zl), 'dp', 0, 0, tiled=True, axis_index_g...  9.87 us
    all_to_all x1, waiting for transfers between devices, on_device(): lax.all_to_all(reorder(partial, zl), 'dp', 0, 0, tiled=True, axis_index_g...  9.45 us
    ppermute x4, starting transfers between devices, on_device(): theirs = [lax.ppermute(block, 'head', CORES) for block in mine]  7.64 us
  transfers between devices with their start and end apart: 12, of which 7 were waited for; matrix products, arithmetic and copies ran while one was open for 5% of the time, Pallas kernels for 0%

profile of v1, /device:TPU:64, one launch (start us, length us, event | category | flops | bytes accessed | tf_op | source)
XLA Modules:
  0.0 178.7 jit_solution(2466488234782974767)
XLA Ops:
  0.6 1.7 broadcast_in_dim.29
  2.4 14.8 %all-to-all-start = ((bf16[16,128,128]{2,1,0:T(8,128)(2,1)}), bf16[16,128,128]{2,1,0:T(8,128)(2,1)S(1)}, u32[]{:S(2)}, u32[]{:S(2)}) async-start(bf16[16,128,128]{2,1,0:T(8,128)(2,1)} %broadcast_in_dim.29), calls=%async_computation | async-start | bytes 1048576 | tf_op jit(solution)/shard_map/all_to_all | solution.py:37
  17.1 3.4 %collective-permute-start.2 = (bf16[256,1024]{1,0:T(8,128)(2,1)}, bf16[256,1024]{1,0:T(8,128)(2,1)S(1)}, u32[]{:S(2)}, u32[]{:S(2)}) collective-permute-start(bf16[256,1024]{1,0:T(8,128)(2,1)} %param.5), channel_id=1, source_target_pairs={{0,2},{1,3},{2,130},{3,131},{4,258},{5,259},{6,386},{7,387},{8,10}... | collective-permute-start | bytes 1572872 | tf_op jit(solution)/shard_map/ppermute | solution.py:89
  20.5 4.3 %collective-permute-start = (bf16[256,1024]{1,0:T(8,128)(2,1)}, bf16[256,1024]{1,0:T(8,128)(2,1)S(1)}, u32[]{:S(2)}, u32[]{:S(2)}) collective-permute-start(bf16[256,1024]{1,0:T(8,128)(2,1)} %param.5), channel_id=1, source_target_pairs={{0,0},{1,1},{2,128},{3,129},{4,256},{5,257},{6,384},{7,385},{8,8},... | collective-permute-start | bytes 1572872 | tf_op jit(solution)/shard_map/ppermute | solution.py:89
  24.8 4.9 %collective-permute-start.6 = (bf16[256,1024]{1,0:T(8,128)(2,1)}, bf16[256,1024]{1,0:T(8,128)(2,1)S(1)}, u32[]{:S(2)}, u32[]{:S(2)}) collective-permute-start(bf16[256,1024]{1,0:T(8,128)(2,1)} %param.5), channel_id=1, source_target_pairs={{0,6},{1,7},{2,134},{3,135},{4,262},{5,263},{6,390},{7,391},{8,14}... | collective-permute-start | bytes 1572872 | tf_op jit(solution)/shard_map/ppermute | solution.py:89
  29.7 4.3 %collective-permute-start.4 = (bf16[256,1024]{1,0:T(8,128)(2,1)}, bf16[256,1024]{1,0:T(8,128)(2,1)}, u32[]{:S(2)}, u32[]{:S(2)}) collective-permute-start(bf16[256,1024]{1,0:T(8,128)(2,1)} %param.5), channel_id=1, source_target_pairs={{0,4},{1,5},{2,132},{3,133},{4,260},{5,261},{6,388},{7,389},{8,12}... | collective-permute-start | bytes 1572872 | tf_op jit(solution)/shard_map/ppermute | solution.py:89
  34.0 10.2 %collective-permute-done.2 = bf16[256,1024]{1,0:T(8,128)(2,1)S(1)} collective-permute-done((bf16[256,1024]{1,0:T(8,128)(2,1)}, bf16[256,1024]{1,0:T(8,128)(2,1)S(1)}, u32[]{:S(2)}, u32[]{:S(2)}) %collective-permute-start.2) | collective-permute-done | bytes 524320 | tf_op jit(solution)/shard_map/ppermute | solution.py:89
  44.2 1.9 %collective-permute-start.3 = (bf16[256,1024]{1,0:T(8,128)(2,1)S(1)}, bf16[256,1024]{1,0:T(8,128)(2,1)}, u32[]{:S(2)}, u32[]{:S(2)}) collective-permute-start(bf16[256,1024]{1,0:T(8,128)(2,1)S(1)} %collective-permute-done.2), channel_id=1, source_target_pairs={{0,1},{1,0},{2,3},{3,2},{4,5},{5,4},{6,7},{7,6},{8,9},{9,8},{10,11... | collective-permute-start | bytes 1572872 | tf_op jit(solution)/shard_map/ppermute | solution.py:92
  46.1 21.5 %collective-permute-done = bf16[256,1024]{1,0:T(8,128)(2,1)S(1)} collective-permute-done((bf16[256,1024]{1,0:T(8,128)(2,1)}, bf16[256,1024]{1,0:T(8,128)(2,1)S(1)}, u32[]{:S(2)}, u32[]{:S(2)}) %collective-permute-start) | collective-permute-done | bytes 524320 | tf_op jit(solution)/shard_map/ppermute | solution.py:89
  67.6 1.9 %collective-permute-start.1 = (bf16[256,1024]{1,0:T(8,128)(2,1)S(1)}, bf16[256,1024]{1,0:T(8,128)(2,1)S(1)}, u32[]{:S(2)}, u32[]{:S(2)}) collective-permute-start(bf16[256,1024]{1,0:T(8,128)(2,1)S(1)} %collective-permute-done), channel_id=1, source_target_pairs={{0,1},{1,0},{2,3},{3,2},{4,5},{5,4},{6,7},{7,6},{8,9},{9,8},{10,11... | collective-permute-start | bytes 1572872 | tf_op jit(solution)/shard_map/ppermute | solution.py:92
  69.5 13.3 %collective-permute-done.6 = bf16[256,1024]{1,0:T(8,128)(2,1)S(1)} collective-permute-done((bf16[256,1024]{1,0:T(8,128)(2,1)}, bf16[256,1024]{1,0:T(8,128)(2,1)S(1)}, u32[]{:S(2)}, u32[]{:S(2)}) %collective-permute-start.6) | collective-permute-done | bytes 524320 | tf_op jit(solution)/shard_map/ppermute | solution.py:89
  82.8 1.9 %collective-permute-start.7 = (bf16[256,1024]{1,0:T(8,128)(2,1)S(1)}, bf16[256,1024]{1,0:T(8,128)(2,1)}, u32[]{:S(2)}, u32[]{:S(2)}) collective-permute-start(bf16[256,1024]{1,0:T(8,128)(2,1)S(1)} %collective-permute-done.6), channel_id=1, source_target_pairs={{0,1},{1,0},{2,3},{3,2},{4,5},{5,4},{6,7},{7,6},{8,9},{9,8},{10,11... | collective-permute-start | bytes 1572872 | tf_op jit(solution)/shard_map/ppermute | solution.py:92
  84.7 5.8 %collective-permute-done.4 = bf16[256,1024]{1,0:T(8,128)(2,1)} collective-permute-done((bf16[256,1024]{1,0:T(8,128)(2,1)}, bf16[256,1024]{1,0:T(8,128)(2,1)}, u32[]{:S(2)}, u32[]{:S(2)}) %collective-permute-start.4) | collective-permute-done | bytes 524320 | tf_op jit(solution)/shard_map/ppermute | solution.py:89
  90.6 1.9 %collective-permute-start.5 = (bf16[256,1024]{1,0:T(8,128)(2,1)}, bf16[256,1024]{1,0:T(8,128)(2,1)}, u32[]{:S(2)}, u32[]{:S(2)}) collective-permute-start(bf16[256,1024]{1,0:T(8,128)(2,1)} %collective-permute-done.4), channel_id=1, source_target_pairs={{0,1},{1,0},{2,3},{3,2},{4,5},{5,4},{6,7},{7,6},{8,9},{9,8},{10,11... | collective-permute-start | bytes 1572872 | tf_op jit(solution)/shard_map/ppermute | solution.py:92
  93.5 1.4 fusion.47
  94.9 1.4 fusion.19
  96.6 1.4 fusion.17
  98.0 1.4 fusion.18
  100.3 9.9 %all-to-all-start.1 = ((f32[4,256,128]{1,2,0:T(8,128)}), f32[4,256,128]{1,2,0:T(8,128)S(1)}, u32[]{:S(2)}, u32[]{:S(2)}) async-start(f32[4,256,128]{1,2,0:T(8,128)} %fusion.30), calls=%async_computation.1 | async-start | bytes 1048576 | tf_op jit(solution)/shard_map/all_to_all | solution.py:101
  110.4 9.5 %all-to-all-done.1 = f32[4,256,128]{1,2,0:T(8,128)S(1)} async-done(((f32[4,256,128]{1,2,0:T(8,128)}), f32[4,256,128]{1,2,0:T(8,128)S(1)}, u32[]{:S(2)}, u32[]{:S(2)}) %all-to-all-start.1) | async-done | bytes 524320 | tf_op jit(solution)/shard_map/all_to_all | solution.py:101
  119.9 2.3 %fusion.83 = (f32[8,256]{1,0:T(8,128)S(1)}, f32[8,256,256]{1,2,0:T(8,128)}) fusion(pred[256,256]{0,1:T(8,128)(4,1)S(1)} %iota_compare_fusion, bf16[256,128]{0,1:T(8,128)(2,1)S(1)} %reduce_sum.36, bf16[256,1024]{1,0:T(8,128)(2,1)S(1)} %copy-done), kind=kOutput, calls=%fused_computation.101 | convolution fusion | flops 136839424 | bytes 2760704 | tf_op jit(solution)/shard_map/sub | solution.py:61
  122.3 1.9 %fusion.27 = bf16[8,256,256]{1,2,0:T(8,128)(2,1)S(1)} fusion(f32[8,256,256]{1,2,0:T(8,128)} %get-tuple-element.13, f32[8,256]{1,0:T(8,128)S(1)} %get-tuple-element.12), kind=kLoop, calls=%fused_computation.44 | loop fusion | flops 1048576 | bytes 3153920 | tf_op jit(solution)/shard_map/convert_element_type | solution.py:63
  127.2 4.0 %all-to-all-start.2 = ((bf16[4,256,128]{2,1,0:T(8,128)(2,1)}), bf16[4,256,128]{2,1,0:T(8,128)(2,1)}, u32[]{:S(2)}, u32[]{:S(2)}) async-start(bf16[4,256,128]{2,1,0:T(8,128)(2,1)} %broadcast_in_dim.33), calls=%async_computation.2 | async-start | bytes 524288 | tf_op jit(solution)/shard_map/all_to_all | solution.py:37
  131.2 6.7 %all-to-all-done.2 = bf16[4,256,128]{2,1,0:T(8,128)(2,1)} async-done(((bf16[4,256,128]{2,1,0:T(8,128)(2,1)}), bf16[4,256,128]{2,1,0:T(8,128)(2,1)}, u32[]{:S(2)}, u32[]{:S(2)}) %all-to-all-start.2) | async-done | bytes 262176 | tf_op jit(solution)/shard_map/all_to_all | solution.py:37
  139.0 1.3 fusion.67
  140.4 1.3 fusion.65
  141.8 1.3 fusion.63
  143.1 1.3 fusion.66
  147.1 11.7 %all-to-all-start.3 = ((bf16[16,128,128]{1,2,0:T(8,128)(2,1)}), bf16[16,128,128]{1,2,0:T(8,128)(2,1)S(1)}, u32[]{:S(2)}, u32[]{:S(2)}) async-start(bf16[16,128,128]{1,2,0:T(8,128)(2,1)} %copy.40), calls=%async_computation.3 | async-start | bytes 1048576 | tf_op jit(solution)/shard_map/all_to_all | solution.py:119
  158.8 1.5 fusion.7
  161.4 1.1 fusion.22
  162.4 15.5 %all-to-all-done.3 = bf16[16,128,128]{1,2,0:T(8,128)(2,1)S(1)} async-done(((bf16[16,128,128]{1,2,0:T(8,128)(2,1)}), bf16[16,128,128]{1,2,0:T(8,128)(2,1)S(1)}, u32[]{:S(2)}, u32[]{:S(2)}) %all-to-all-start.3) | async-done | bytes 524320 | tf_op jit(solution)/shard_map/all_to_all | solution.py:119
  (49 shorter events, 11.0 us)
Async XLA Ops:
  0.6 119.3 %copy-start = (bf16[256,1024]{1,0:T(8,128)(2,1)S(1)}, bf16[256,1024]{1,0:T(8,128)(2,1)}, u32[]{:S(2)}) copy-start(bf16[256,1024]{1,0:T(8,128)(2,1)} %param.7) | copy-start | bytes 1572868
  2.4 90.1 %all-to-all-start = ((bf16[16,128,128]{2,1,0:T(8,128)(2,1)}), bf16[16,128,128]{2,1,0:T(8,128)(2,1)S(1)}, u32[]{:S(2)}, u32[]{:S(2)}) async-start(bf16[16,128,128]{2,1,0:T(8,128)(2,1)} %broadcast_in_dim.29), calls=%async_computation | async-start | bytes 1048576 | tf_op jit(solution)/shard_map/all_to_all | solution.py:37
  17.1 27.1 %collective-permute-start.2 = (bf16[256,1024]{1,0:T(8,128)(2,1)}, bf16[256,1024]{1,0:T(8,128)(2,1)S(1)}, u32[]{:S(2)}, u32[]{:S(2)}) collective-permute-start(bf16[256,1024]{1,0:T(8,128)(2,1)} %param.5), channel_id=1, source_target_pairs={{0,2},{1,3},{2,130},{3,131},{4,258},{5,259},{6,386},{7,387},{8,10}... | collective-permute-start | bytes 1572872 | tf_op jit(solution)/shard_map/ppermute | solution.py:89
  20.5 47.1 %collective-permute-start = (bf16[256,1024]{1,0:T(8,128)(2,1)}, bf16[256,1024]{1,0:T(8,128)(2,1)S(1)}, u32[]{:S(2)}, u32[]{:S(2)}) collective-permute-start(bf16[256,1024]{1,0:T(8,128)(2,1)} %param.5), channel_id=1, source_target_pairs={{0,0},{1,1},{2,128},{3,129},{4,256},{5,257},{6,384},{7,385},{8,8},... | collective-permute-start | bytes 1572872 | tf_op jit(solution)/shard_map/ppermute | solution.py:89
  24.8 58.0 %collective-permute-start.6 = (bf16[256,1024]{1,0:T(8,128)(2,1)}, bf16[256,1024]{1,0:T(8,128)(2,1)S(1)}, u32[]{:S(2)}, u32[]{:S(2)}) collective-permute-start(bf16[256,1024]{1,0:T(8,128)(2,1)} %param.5), channel_id=1, source_target_pairs={{0,6},{1,7},{2,134},{3,135},{4,262},{5,263},{6,390},{7,391},{8,14}... | collective-permute-start | bytes 1572872 | tf_op jit(solution)/shard_map/ppermute | solution.py:89
  29.7 60.9 %collective-permute-start.4 = (bf16[256,1024]{1,0:T(8,128)(2,1)}, bf16[256,1024]{1,0:T(8,128)(2,1)}, u32[]{:S(2)}, u32[]{:S(2)}) collective-permute-start(bf16[256,1024]{1,0:T(8,128)(2,1)} %param.5), channel_id=1, source_target_pairs={{0,4},{1,5},{2,132},{3,133},{4,260},{5,261},{6,388},{7,389},{8,12}... | collective-permute-start | bytes 1572872 | tf_op jit(solution)/shard_map/ppermute | solution.py:89
  44.2 52.0 %copy-start.2 = (bf16[256,1024]{1,0:T(8,128)(2,1)}, bf16[256,1024]{1,0:T(8,128)(2,1)S(1)}, u32[]{:S(2)}) copy-start(bf16[256,1024]{1,0:T(8,128)(2,1)S(1)} %collective-permute-done.2) | copy-start | bytes 1572868
  44.2 50.7 %collective-permute-start.3 = (bf16[256,1024]{1,0:T(8,128)(2,1)S(1)}, bf16[256,1024]{1,0:T(8,128)(2,1)}, u32[]{:S(2)}, u32[]{:S(2)}) collective-permute-start(bf16[256,1024]{1,0:T(8,128)(2,1)S(1)} %collective-permute-done.2), channel_id=1, source_target_pairs={{0,1},{1,0},{2,3},{3,2},{4,5},{5,4},{6,7},{7,6},{8,9},{9,8},{10,11... | collective-permute-start | bytes 1572872 | tf_op jit(solution)/shard_map/ppermute | solution.py:92
  67.6 28.6 %collective-permute-start.1 = (bf16[256,1024]{1,0:T(8,128)(2,1)S(1)}, bf16[256,1024]{1,0:T(8,128)(2,1)S(1)}, u32[]{:S(2)}, u32[]{:S(2)}) collective-permute-start(bf16[256,1024]{1,0:T(8,128)(2,1)S(1)} %collective-permute-done), channel_id=1, source_target_pairs={{0,1},{1,0},{2,3},{3,2},{4,5},{5,4},{6,7},{7,6},{8,9},{9,8},{10,11... | collective-permute-start | bytes 1572872 | tf_op jit(solution)/shard_map/ppermute | solution.py:92
  82.8 13.4 %copy-start.4 = (bf16[256,1024]{1,0:T(8,128)(2,1)}, bf16[256,1024]{1,0:T(8,128)(2,1)S(1)}, u32[]{:S(2)}) copy-start(bf16[256,1024]{1,0:T(8,128)(2,1)S(1)} %collective-permute-done.6) | copy-start | bytes 1572868
  82.8 13.8 %collective-permute-start.7 = (bf16[256,1024]{1,0:T(8,128)(2,1)S(1)}, bf16[256,1024]{1,0:T(8,128)(2,1)}, u32[]{:S(2)}, u32[]{:S(2)}) collective-permute-start(bf16[256,1024]{1,0:T(8,128)(2,1)S(1)} %collective-permute-done.6), channel_id=1, source_target_pairs={{0,1},{1,0},{2,3},{3,2},{4,5},{5,4},{6,7},{7,6},{8,9},{9,8},{10,11... | collective-permute-start | bytes 1572872 | tf_op jit(solution)/shard_map/ppermute | solution.py:92
  90.6 7.4 %collective-permute-start.5 = (bf16[256,1024]{1,0:T(8,128)(2,1)}, bf16[256,1024]{1,0:T(8,128)(2,1)}, u32[]{:S(2)}, u32[]{:S(2)}) collective-permute-start(bf16[256,1024]{1,0:T(8,128)(2,1)} %collective-permute-done.4), channel_id=1, source_target_pairs={{0,1},{1,0},{2,3},{3,2},{4,5},{5,4},{6,7},{7,6},{8,9},{9,8},{10,11... | collective-permute-start | bytes 1572872 | tf_op jit(solution)/shard_map/ppermute | solution.py:92
  99.3 10.9 %copy-start.7 = (bf16[256,1024]{1,0:T(8,128)(2,1)S(1)}, bf16[256,1024]{1,0:T(8,128)(2,1)}, u32[]{:S(2)}) copy-start(bf16[256,1024]{1,0:T(8,128)(2,1)} %param.9) | copy-start | bytes 1572868
  100.3 19.6 %all-to-all-start.1 = ((f32[4,256,128]{1,2,0:T(8,128)}), f32[4,256,128]{1,2,0:T(8,128)S(1)}, u32[]{:S(2)}, u32[]{:S(2)}) async-start(f32[4,256,128]{1,2,0:T(8,128)} %fusion.30), calls=%async_computation.1 | async-start | bytes 1048576 | tf_op jit(solution)/shard_map/all_to_all | solution.py:101
  122.3 1.9 %copy-start.8 = (bf16[256,128]{1,0:T(8,128)(2,1)S(1)}, bf16[256,128]{1,0:T(8,128)(2,1)}, u32[]{:S(2)}) copy-start(bf16[256,128]{1,0:T(8,128)(2,1)} %param.8) | copy-start | bytes 196612
  122.3 2.3 %copy-start.1 = (f32[8,256,256]{1,2,0:T(8,128)S(1)}, f32[8,256,256]{1,2,0:T(8,128)}, u32[]{:S(2)}) copy-start(f32[8,256,256]{1,2,0:T(8,128)} %get-tuple-element.13) | copy-start | bytes 6291460
  125.0 1.0 copy-start.6
  127.2 10.8 %all-to-all-start.2 = ((bf16[4,256,128]{2,1,0:T(8,128)(2,1)}), bf16[4,256,128]{2,1,0:T(8,128)(2,1)}, u32[]{:S(2)}, u32[]{:S(2)}) async-start(bf16[4,256,128]{2,1,0:T(8,128)(2,1)} %broadcast_in_dim.33), calls=%async_computation.2 | async-start | bytes 524288 | tf_op jit(solution)/shard_map/all_to_all | solution.py:37
  139.0 5.3 %copy-start.3 = (bf16[256,1024]{1,0:T(8,128)(2,1)S(1)}, bf16[256,1024]{1,0:T(8,128)(2,1)}, u32[]{:S(2)}) copy-start(bf16[256,1024]{1,0:T(8,128)(2,1)} %copy-done.2) | copy-start | bytes 1572868
  140.4 4.2 %copy-start.5 = (bf16[256,1024]{1,0:T(8,128)(2,1)S(1)}, bf16[256,1024]{1,0:T(8,128)(2,1)}, u32[]{:S(2)}) copy-start(bf16[256,1024]{1,0:T(8,128)(2,1)} %copy-done.4) | copy-start | bytes 1572868
  147.1 30.8 %all-to-all-start.3 = ((bf16[16,128,128]{1,2,0:T(8,128)(2,1)}), bf16[16,128,128]{1,2,0:T(8,128)(2,1)S(1)}, u32[]{:S(2)}, u32[]{:S(2)}) async-start(bf16[16,128,128]{1,2,0:T(8,128)(2,1)} %copy.40), calls=%async_computation.3 | async-start | bytes 1048576 | tf_op jit(solution)/shard_map/all_to_all | solution.py:119

commit v2 on v1

--- a/solution.py
+++ b/solution.py
@@ -22,25 +22,41 @@
     for zl in range(ZL)
     for c in range(C)
 ]
-ALONG_X = [[dp_of(x, y, zh) for x in range(X)] for y in range(Y) for zh in range(ZH)]
-ALONG_YZ = [[dp_of(x, y, zh) for y in range(Y) for zh in range(ZH)] for x in range(X)]
 CORES = [(h, h ^ 1) for h in range(ZL * C)]
 
 
-def turned(j):
-    return [(place(x, y, zh, zl, c), place(zl, y, zh, x + j, c)) for x, y, zh, zl, c in CHIPS]
+ALONG_Y = [[dp_of(x, y, zh) for y in range(Y)] for x in range(X) for zh in range(ZH)]
+BOTH = ("dp", "head")
 
 
-def spread(block, groups):
-    n = len(groups[0])
-    many = jnp.broadcast_to(block[None], (n,) + block.shape)
-    return lax.all_to_all(many, "dp", 0, 0, tiled=True, axis_index_groups=groups)
+def along_x(d):
+    return [(place(x, y, zh, zl, c), place(x + d, y, zh, zl, c)) for x, y, zh, zl, c in CHIPS]
 
 
-def reorder(parts, zl):
+def to_owner(k):
+    return [(place(x, y, zh, zl, c), place(zl + k, y, zh, x, c)) for x, y, zh, zl, c in CHIPS]
+
+
+def from_owner(k):
+    return [(b, a) for a, b in to_owner(k)]
+
+
+def turned(flip):
+    return [(place(x, y, zh, zl, c), place(zl, y, zh ^ flip, x, c)) for x, y, zh, zl, c in CHIPS]
+
+
+def send(block, pairs):
+    return lax.ppermute(block, BOTH, pairs)
+
+
+def reorder(parts, first):
     back = parts[::-1]
     twice = jnp.concatenate([back, back], axis=0)
-    return lax.dynamic_slice_in_dim(twice, X - 1 - zl, X, axis=0)
+    return lax.dynamic_slice_in_dim(twice, X - 1 - first, X, axis=0)
+
+
+def in_order(own, other, position):
+    return jnp.where(position == 0, jnp.stack([own, other]), jnp.stack([other, own]))
 
 
 def attention(queries, keys, values, out_grad):
@@ -82,13 +98,19 @@
 
 
 def on_device(tokens, key_weight, queries, values, out_grad):
-    f32 = jnp.float32
+    f32, bf16 = jnp.float32, jnp.bfloat16
     length, feats = tokens.shape
-    head = lax.axis_index("head")
+    rows, width = key_weight.shape
+    dp, head = lax.axis_index("dp"), lax.axis_index("head")
+    x, zh = dp // (Y * ZH), dp % ZH
     zl, c = head // C, head % C
-    mine = [lax.ppermute(tokens, ("dp", "head"), turned(j)) for j in range(X)]
-    weight = spread(key_weight, ALONG_YZ).reshape(C * feats, -1)
-    width = weight.shape[1]
+    first = (x - zl) % X
+
+    weight = in_order(*(send(key_weight, turned(flip)) for flip in range(ZH)), zh)
+    mine = [tokens] + [send(tokens, along_x(d)) for d in range(1, X)]
+    weight = jnp.broadcast_to(weight[None], (Y, ZH, rows, width))
+    weight = lax.all_to_all(weight, "dp", 0, 0, tiled=True, axis_index_groups=ALONG_Y)
+    weight = weight.reshape(C * feats, width)
     theirs = [lax.ppermute(block, "head", CORES) for block in mine]
     near = lax.dynamic_slice_in_dim(weight, c * feats, feats, axis=0)
     far = lax.dynamic_slice_in_dim(weight, (1 - c) * feats, feats, axis=0)
@@ -98,28 +120,29 @@
             for a, b in zip(mine, theirs)
         ]
     )
-    partial = lax.all_to_all(
-        reorder(partial, zl), "dp", 0, 0, tiled=True, axis_index_groups=ALONG_X
-    )
-    keys = jnp.sum(partial, axis=0).astype(jnp.bfloat16)
+    partial = reorder(partial, first)
+    keys = sum(send(partial[k], to_owner(k)) for k in range(X)).astype(bf16)
     query_grad, key_grad, value_grad = attention(queries, keys, values, out_grad)
-    grads = reorder(spread(key_grad, ALONG_X).reshape(X, length, width), zl)
+    grads = reorder(jnp.stack([send(key_grad, from_owner(k)) for k in range(X)]), first)
 
     def contracted(blocks):
         return sum(
             lax.dot_general(
-                a, grads[j], (((0,), (0,)), ((), ())), preferred_element_type=f32
+                a, grads[d], (((0,), (0,)), ((), ())), preferred_element_type=f32
             )
-            for j, a in enumerate(blocks)
+            for d, a in enumerate(blocks)
         )
 
     own, other = contracted(mine), contracted(theirs)
-    rows = jnp.concatenate([own, other, own], axis=0).astype(jnp.bfloat16)
-    rows = lax.dynamic_slice_in_dim(rows, c * feats, C * feats, axis=0)
-    rows = lax.all_to_all(
-        rows.reshape(Y * ZH, -1, width), "dp", 0, 0, tiled=True, axis_index_groups=ALONG_YZ
+    total = jnp.concatenate([own, other, own], axis=0).astype(bf16)
+    total = lax.dynamic_slice_in_dim(total, c * feats, C * feats, axis=0)
+    total = lax.all_to_all(
+        total.reshape(Y, ZH * rows, width), "dp", 0, 0, tiled=True, axis_index_groups=ALONG_Y
     )
-    weight_grad = jnp.sum(rows.astype(f32), axis=0)
+    total = jnp.sum(total.astype(f32), axis=0).astype(bf16).reshape(ZH, rows, width)
+    stays = lax.dynamic_index_in_dim(total, zh, 0, keepdims=False)
+    leaves = lax.dynamic_index_in_dim(total, 1 - zh, 0, keepdims=False)
+    weight_grad = send(stays, turned(0)).astype(f32) + send(leaves, turned(1)).astype(f32)
     return query_grad, value_grad, weight_grad
 
 

time: 180 us -> 183 us (1.017)
  the two profiles are of different devices: /device:TPU:64 before, /device:TPU:4 now
where the time goes in v2:
time: 183 us; the launch traced here: 181 us
  starting transfers between devices  93.5 us (51%)
  waiting for transfers between devices  55.9 us (31%)
  matrix products  20.1 us (11%)
  local copies, waits for them, and re-layouts  6.52 us (4%)
  other arithmetic  4.06 us (2%)
    ppermute x15, starting transfers between devices, send(): return lax.ppermute(block, BOTH, pairs)  71.3 us
    ppermute x15, waiting for transfers between devices, send(): return lax.ppermute(block, BOTH, pairs)  41.3 us
    all_to_all x1, waiting for transfers between devices, on_device(): lax.all_to_all(total.reshape(Y, ZH * rows, width), 'dp', 0, 0, tiled=True...  14.6 us
    ppermute x4, starting transfers between devices, on_device(): theirs = [lax.ppermute(block, 'head', CORES) for block in mine]  8.15 us
    dot_general x8, matrix products, contracted(): lax.dot_general(a, grads[d], (((0,), (0,)), ((), ())), preferred_element_...  7.27 us
    all_to_all x1, starting transfers between devices, on_device(): lax.all_to_all(weight, 'dp', 0, 0, tiled=True, axis_index_groups=ALONG_Y)  7.1 us
    all_to_all x1, starting transfers between devices, on_device(): lax.all_to_all(total.reshape(Y, ZH * rows, width), 'dp', 0, 0, tiled=True...  6.92 us
    dot_general x4, matrix products, on_device(): jnp.dot(b, far, preferred_element_type=f32)  4.4 us
  transfers between devices with their start and end apart: 21, of which 7 were waited for; matrix products, arithmetic and copies ran while one was open for 5% of the time, Pallas kernels for 0%

profile of v2, /device:TPU:4, one launch (start us, length us, event | category | flops | bytes accessed | tf_op | source)
XLA Modules:
  0.0 181.5 jit_solution(4688240567543750153)
XLA Ops:
  0.7 11.0 %collective-permute-start.1 = (bf16[128,128]{1,0:T(8,128)(2,1)}, bf16[128,128]{1,0:T(8,128)(2,1)S(1)}, u32[]{:S(2)}, u32[]{:S(2)}) collective-permute-start(bf16[128,128]{1,0:T(8,128)(2,1)} %param.6), channel_id=1, source_target_pairs={{0,8},{1,9},{2,136},{3,137},{4,264},{5,265},{6,392},{7,393},{8,0},... | collective-permute-start | bytes 98312 | tf_op jit(solution)/shard_map/ppermute | solution.py:49
  11.7 4.9 %collective-permute-start = (bf16[128,128]{1,0:T(8,128)(2,1)}, bf16[128,128]{1,0:T(8,128)(2,1)S(1)}, u32[]{:S(2)}, u32[]{:S(2)}) collective-permute-start(bf16[128,128]{1,0:T(8,128)(2,1)} %param.6), channel_id=1, source_target_pairs={{0,0},{1,1},{2,128},{3,129},{4,256},{5,257},{6,384},{7,385},{8,8},... | collective-permute-start | bytes 98312 | tf_op jit(solution)/shard_map/ppermute | solution.py:49
  16.6 4.4 %collective-permute-done = bf16[128,128]{1,0:T(8,128)(2,1)S(1)} collective-permute-done((bf16[128,128]{1,0:T(8,128)(2,1)}, bf16[128,128]{1,0:T(8,128)(2,1)S(1)}, u32[]{:S(2)}, u32[]{:S(2)}) %collective-permute-start) | collective-permute-done | bytes 32800 | tf_op jit(solution)/shard_map/ppermute | solution.py:49
  21.9 7.1 %all-to-all-start = ((bf16[8,2,128,128]{3,2,1,0:T(8,128)(2,1)}), bf16[8,2,128,128]{3,2,1,0:T(8,128)(2,1)S(1)}, u32[]{:S(2)}, u32[]{:S(2)}) async-start(bf16[8,2,128,128]{3,2,1,0:T(8,128)(2,1)} %broadcast_in_dim.23), calls=%async_computation | async-start | bytes 1048576 | tf_op jit(solution)/shard_map/all_to_all | solution.py:112
  29.0 1.9 %collective-permute-start.5 = (bf16[256,1024]{1,0:T(8,128)(2,1)}, bf16[256,1024]{1,0:T(8,128)(2,1)}, u32[]{:S(2)}, u32[]{:S(2)}) collective-permute-start(bf16[256,1024]{1,0:T(8,128)(2,1)} %param.5), channel_id=1, source_target_pairs={{0,256},{1,257},{2,258},{3,259},{4,260},{5,261},{6,262},{7,263},{8... | collective-permute-start | bytes 1572872 | tf_op jit(solution)/shard_map/ppermute | solution.py:49
  30.9 3.7 %collective-permute-start.3 = (bf16[256,1024]{1,0:T(8,128)(2,1)}, bf16[256,1024]{1,0:T(8,128)(2,1)S(1)}, u32[]{:S(2)}, u32[]{:S(2)}) collective-permute-start(bf16[256,1024]{1,0:T(8,128)(2,1)} %param.5), channel_id=1, source_target_pairs={{0,128},{1,129},{2,130},{3,131},{4,132},{5,133},{6,134},{7,135},{8... | collective-permute-start | bytes 1572872 | tf_op jit(solution)/shard_map/ppermute | solution.py:49
  34.6 3.4 %collective-permute-start.7 = (bf16[256,1024]{1,0:T(8,128)(2,1)}, bf16[256,1024]{1,0:T(8,128)(2,1)S(1)}, u32[]{:S(2)}, u32[]{:S(2)}) collective-permute-start(bf16[256,1024]{1,0:T(8,128)(2,1)} %param.5), channel_id=1, source_target_pairs={{0,384},{1,385},{2,386},{3,387},{4,388},{5,389},{6,390},{7,391},{8... | collective-permute-start | bytes 1572872 | tf_op jit(solution)/shard_map/ppermute | solution.py:49
  38.0 1.9 %collective-permute-start.2 = (bf16[256,1024]{1,0:T(8,128)(2,1)}, bf16[256,1024]{1,0:T(8,128)(2,1)}, u32[]{:S(2)}, u32[]{:S(2)}) collective-permute-start(bf16[256,1024]{1,0:T(8,128)(2,1)} %param.5), channel_id=1, source_target_pairs={{0,1},{1,0},{2,3},{3,2},{4,5},{5,4},{6,7},{7,6},{8,9},{9,8},{10,11... | collective-permute-start | bytes 1572872 | tf_op jit(solution)/shard_map/ppermute | solution.py:114
  40.0 7.5 %collective-permute-done.5 = bf16[256,1024]{1,0:T(8,128)(2,1)} collective-permute-done((bf16[256,1024]{1,0:T(8,128)(2,1)}, bf16[256,1024]{1,0:T(8,128)(2,1)}, u32[]{:S(2)}, u32[]{:S(2)}) %collective-permute-start.5) | collective-permute-done | bytes 524320 | tf_op jit(solution)/shard_map/ppermute | solution.py:49
  47.6 1.9 %collective-permute-start.6 = (bf16[256,1024]{1,0:T(8,128)(2,1)}, bf16[256,1024]{1,0:T(8,128)(2,1)}, u32[]{:S(2)}, u32[]{:S(2)}) collective-permute-start(bf16[256,1024]{1,0:T(8,128)(2,1)} %collective-permute-done.5), channel_id=1, source_target_pairs={{0,1},{1,0},{2,3},{3,2},{4,5},{5,4},{6,7},{7,6},{8,9},{9,8},{10,11... | collective-permute-start | bytes 1572872 | tf_op jit(solution)/shard_map/ppermute | solution.py:114
  49.5 6.3 %collective-permute-done.3 = bf16[256,1024]{1,0:T(8,128)(2,1)S(1)} collective-permute-done((bf16[256,1024]{1,0:T(8,128)(2,1)}, bf16[256,1024]{1,0:T(8,128)(2,1)S(1)}, u32[]{:S(2)}, u32[]{:S(2)}) %collective-permute-start.3) | collective-permute-done | bytes 524320 | tf_op jit(solution)/shard_map/ppermute | solution.py:49
  55.8 1.9 %collective-permute-start.4 = (bf16[256,1024]{1,0:T(8,128)(2,1)S(1)}, bf16[256,1024]{1,0:T(8,128)(2,1)S(1)}, u32[]{:S(2)}, u32[]{:S(2)}) collective-permute-start(bf16[256,1024]{1,0:T(8,128)(2,1)S(1)} %collective-permute-done.3), channel_id=1, source_target_pairs={{0,1},{1,0},{2,3},{3,2},{4,5},{5,4},{6,7},{7,6},{8,9},{9,8},{10,11... | collective-permute-start | bytes 1572872 | tf_op jit(solution)/shard_map/ppermute | solution.py:114
  57.7 2.4 %collective-permute-start.8 = (bf16[256,1024]{1,0:T(8,128)(2,1)S(1)}, bf16[256,1024]{1,0:T(8,128)(2,1)}, u32[]{:S(2)}, u32[]{:S(2)}) collective-permute-start(bf16[256,1024]{1,0:T(8,128)(2,1)S(1)} %collective-permute-done.7), channel_id=1, source_target_pairs={{0,1},{1,0},{2,3},{3,2},{4,5},{5,4},{6,7},{7,6},{8,9},{9,8},{10,11... | collective-permute-start | bytes 1572872 | tf_op jit(solution)/shard_map/ppermute | solution.py:114
  63.9 1.4 fusion.16
  67.9 2.4 %collective-permute-start.10 = (f32[256,128]{0,1:T(8,128)}, f32[256,128]{0,1:T(8,128)S(1)}, u32[]{:S(2)}, u32[]{:S(2)}) collective-permute-start(f32[256,128]{0,1:T(8,128)} %get-tuple-element.12), channel_id=1, source_target_pairs={{0,128},{1,129},{2,256},{3,257},{4,384},{5,385},{6,0},{7,1},{8,136... | collective-permute-start | bytes 393224 | tf_op jit(solution)/shard_map/ppermute | solution.py:49
  70.3 3.6 %collective-permute-start.11 = (f32[256,128]{0,1:T(8,128)S(1)}, f32[256,128]{0,1:T(8,128)S(1)}, u32[]{:S(2)}, u32[]{:S(2)}) collective-permute-start(f32[256,128]{0,1:T(8,128)S(1)} %get-tuple-element.13), channel_id=1, source_target_pairs={{0,256},{1,257},{2,384},{3,385},{4,0},{5,1},{6,128},{7,129},{8,264... | collective-permute-start | bytes 393224 | tf_op jit(solution)/shard_map/ppermute | solution.py:49
  73.9 4.1 %collective-permute-start.9 = (f32[256,128]{0,1:T(8,128)S(1)}, f32[256,128]{0,1:T(8,128)S(1)}, u32[]{:S(2)}, u32[]{:S(2)}) collective-permute-start(f32[256,128]{0,1:T(8,128)S(1)} %get-tuple-element.14), channel_id=1, source_target_pairs={{0,0},{1,1},{2,128},{3,129},{4,256},{5,257},{6,384},{7,385},{8,8},... | collective-permute-start | bytes 393224 | tf_op jit(solution)/shard_map/ppermute | solution.py:49
  78.1 3.5 %collective-permute-start.12 = (f32[256,128]{0,1:T(8,128)S(1)}, f32[256,128]{0,1:T(8,128)S(1)}, u32[]{:S(2)}, u32[]{:S(2)}) collective-permute-start(f32[256,128]{0,1:T(8,128)S(1)} %get-tuple-element.15), channel_id=1, source_target_pairs={{0,384},{1,385},{2,0},{3,1},{4,128},{5,129},{6,256},{7,257},{8,392... | collective-permute-start | bytes 393224 | tf_op jit(solution)/shard_map/ppermute | solution.py:49
  81.9 17.8 %collective-permute-done.10 = f32[256,128]{0,1:T(8,128)S(1)} collective-permute-done((f32[256,128]{0,1:T(8,128)}, f32[256,128]{0,1:T(8,128)S(1)}, u32[]{:S(2)}, u32[]{:S(2)}) %collective-permute-start.10) | collective-permute-done | bytes 131104 | tf_op jit(solution)/shard_map/ppermute | solution.py:49
  99.7 2.3 %fusion.70 = (f32[8,256]{1,0:T(8,128)S(1)}, f32[8,256,256]{1,2,0:T(8,128)}) fusion(pred[256,256]{0,1:T(8,128)(4,1)S(1)} %iota_compare_fusion, bf16[256,128,1]{0,1,2:T(8,128)(2,1)S(1)} %fusion.51, bf16[256,1024]{1,0:T(8,128)(2,1)S(1)} %copy-done), kind=kOutput, calls=%fused_computation.103 | convolution fusion | flops 136839424 | bytes 2760704 | tf_op jit(solution)/shard_map/sub | solution.py:77
  102.0 1.9 %fusion.25 = bf16[8,256,256]{1,2,0:T(8,128)(2,1)S(1)} fusion(f32[8,256,256]{1,2,0:T(8,128)} %get-tuple-element.19, f32[8,256]{1,0:T(8,128)S(1)} %get-tuple-element.18), kind=kLoop, calls=%fused_computation.43 | loop fusion | flops 1048576 | bytes 3153920 | tf_op jit(solution)/shard_map/convert_element_type | solution.py:79
  106.2 7.0 %collective-permute-start.16 = (bf16[256,128]{1,0:T(8,128)(2,1)S(1)}, bf16[256,128]{1,0:T(8,128)(2,1)S(1)}, u32[]{:S(2)}, u32[]{:S(2)}) collective-permute-start(bf16[256,128]{1,0:T(8,128)(2,1)S(1)} %fusion.21), channel_id=1, source_target_pairs={{384,0},{385,1},{0,2},{1,3},{128,4},{129,5},{256,6},{257,7},{392,8... | collective-permute-start | bytes 196616 | tf_op jit(solution)/shard_map/ppermute | solution.py:49
  113.3 5.7 %collective-permute-start.15 = (bf16[256,128]{1,0:T(8,128)(2,1)S(1)}, bf16[256,128]{1,0:T(8,128)(2,1)S(1)}, u32[]{:S(2)}, u32[]{:S(2)}) collective-permute-start(bf16[256,128]{1,0:T(8,128)(2,1)S(1)} %fusion.21), channel_id=1, source_target_pairs={{256,0},{257,1},{384,2},{385,3},{0,4},{1,5},{128,6},{129,7},{264,8... | collective-permute-start | bytes 196616 | tf_op jit(solution)/shard_map/ppermute | solution.py:49
  118.9 1.9 %collective-permute-start.14 = (bf16[256,128]{1,0:T(8,128)(2,1)S(1)}, bf16[256,128]{1,0:T(8,128)(2,1)S(1)}, u32[]{:S(2)}, u32[]{:S(2)}) collective-permute-start(bf16[256,128]{1,0:T(8,128)(2,1)S(1)} %fusion.21), channel_id=1, source_target_pairs={{128,0},{129,1},{256,2},{257,3},{384,4},{385,5},{0,6},{1,7},{136,8... | collective-permute-start | bytes 196616 | tf_op jit(solution)/shard_map/ppermute | solution.py:49
  120.9 9.3 %collective-permute-start.13 = (bf16[256,128]{1,0:T(8,128)(2,1)S(1)}, bf16[256,128]{1,0:T(8,128)(2,1)S(1)}, u32[]{:S(2)}, u32[]{:S(2)}) collective-permute-start(bf16[256,128]{1,0:T(8,128)(2,1)S(1)} %fusion.21), channel_id=1, source_target_pairs={{0,0},{1,1},{128,2},{129,3},{256,4},{257,5},{384,6},{385,7},{8,8},... | collective-permute-start | bytes 196616 | tf_op jit(solution)/shard_map/ppermute | solution.py:49
  130.2 2.5 %collective-permute-done.13 = bf16[256,128]{1,0:T(8,128)(2,1)S(1)} collective-permute-done((bf16[256,128]{1,0:T(8,128)(2,1)S(1)}, bf16[256,128]{1,0:T(8,128)(2,1)S(1)}, u32[]{:S(2)}, u32[]{:S(2)}) %collective-permute-start.13) | collective-permute-done | bytes 65568 | tf_op jit(solution)/shard_map/ppermute | solution.py:49
  143.5 6.9 %all-to-all-start.1 = ((bf16[8,256,128]{1,2,0:T(8,128)(2,1)}), bf16[8,256,128]{1,2,0:T(8,128)(2,1)S(1)}, u32[]{:S(2)}, u32[]{:S(2)}) async-start(bf16[8,256,128]{1,2,0:T(8,128)(2,1)} %copy.41), calls=%async_computation.1 | async-start | bytes 1048576 | tf_op jit(solution)/shard_map/all_to_all | solution.py:139
  151.5 14.6 %all-to-all-done.1 = bf16[8,256,128]{1,2,0:T(8,128)(2,1)S(1)} async-done(((bf16[8,256,128]{1,2,0:T(8,128)(2,1)}), bf16[8,256,128]{1,2,0:T(8,128)(2,1)S(1)}, u32[]{:S(2)}, u32[]{:S(2)}) %all-to-all-start.1) | async-done | bytes 524320 | tf_op jit(solution)/shard_map/all_to_all | solution.py:139
  166.6 5.1 %collective-permute-start.18 = (bf16[128,128]{1,0:T(8,128)(2,1)S(1)}, bf16[128,128]{1,0:T(8,128)(2,1)S(1)}, u32[]{:S(2)}, u32[]{:S(2)}) collective-permute-start(bf16[128,128]{1,0:T(8,128)(2,1)S(1)} %bitcast.162), channel_id=1, source_target_pairs={{0,8},{1,9},{2,136},{3,137},{4,264},{5,265},{6,392},{7,393},{8,0},... | collective-permute-start | bytes 98312 | tf_op jit(solution)/shard_map/ppermute | solution.py:49
  171.7 3.8 %collective-permute-start.17 = (bf16[128,128]{1,0:T(8,128)(2,1)S(1)}, bf16[128,128]{1,0:T(8,128)(2,1)S(1)}, u32[]{:S(2)}, u32[]{:S(2)}) collective-permute-start(bf16[128,128]{1,0:T(8,128)(2,1)S(1)} %bitcast.161), channel_id=1, source_target_pairs={{0,0},{1,1},{2,128},{3,129},{4,256},{5,257},{6,384},{7,385},{8,8},... | collective-permute-start | bytes 98312 | tf_op jit(solution)/shard_map/ppermute | solution.py:49
  175.5 1.5 fusion.7
  178.0 2.8 %collective-permute-done.17 = bf16[128,128]{1,0:T(8,128)(2,1)S(1)} collective-permute-done((bf16[128,128]{1,0:T(8,128)(2,1)S(1)}, bf16[128,128]{1,0:T(8,128)(2,1)S(1)}, u32[]{:S(2)}, u32[]{:S(2)}) %collective-permute-start.17) | collective-permute-done | bytes 32800 | tf_op jit(solution)/shard_map/ppermute | solution.py:49
  (71 shorter events, 23.6 us)
Async XLA Ops:
  0.6 99.1 %copy-start = (bf16[256,1024]{1,0:T(8,128)(2,1)S(1)}, bf16[256,1024]{1,0:T(8,128)(2,1)}, u32[]{:S(2)}) copy-start(bf16[256,1024]{1,0:T(8,128)(2,1)} %param.7) | copy-start | bytes 1572868
  0.6 59.5 %copy-start.2 = (bf16[256,1024]{1,0:T(8,128)(2,1)S(1)}, bf16[256,1024]{1,0:T(8,128)(2,1)}, u32[]{:S(2)}) copy-start(bf16[256,1024]{1,0:T(8,128)(2,1)} %param.5) | copy-start | bytes 1572868
  0.7 16.0 %collective-permute-start.1 = (bf16[128,128]{1,0:T(8,128)(2,1)}, bf16[128,128]{1,0:T(8,128)(2,1)S(1)}, u32[]{:S(2)}, u32[]{:S(2)}) collective-permute-start(bf16[128,128]{1,0:T(8,128)(2,1)} %param.6), channel_id=1, source_target_pairs={{0,8},{1,9},{2,136},{3,137},{4,264},{5,265},{6,392},{7,393},{8,0},... | collective-permute-start | bytes 98312 | tf_op jit(solution)/shard_map/ppermute | solution.py:49
  11.7 9.3 %collective-permute-start = (bf16[128,128]{1,0:T(8,128)(2,1)}, bf16[128,128]{1,0:T(8,128)(2,1)S(1)}, u32[]{:S(2)}, u32[]{:S(2)}) collective-permute-start(bf16[128,128]{1,0:T(8,128)(2,1)} %param.6), channel_id=1, source_target_pairs={{0,0},{1,1},{2,128},{3,129},{4,256},{5,257},{6,384},{7,385},{8,8},... | collective-permute-start | bytes 98312 | tf_op jit(solution)/shard_map/ppermute | solution.py:49
  21.9 38.2 %all-to-all-start = ((bf16[8,2,128,128]{3,2,1,0:T(8,128)(2,1)}), bf16[8,2,128,128]{3,2,1,0:T(8,128)(2,1)S(1)}, u32[]{:S(2)}, u32[]{:S(2)}) async-start(bf16[8,2,128,128]{3,2,1,0:T(8,128)(2,1)} %broadcast_in_dim.23), calls=%async_computation | async-start | bytes 1048576 | tf_op jit(solution)/shard_map/all_to_all | solution.py:112
  29.0 18.5 %collective-permute-start.5 = (bf16[256,1024]{1,0:T(8,128)(2,1)}, bf16[256,1024]{1,0:T(8,128)(2,1)}, u32[]{:S(2)}, u32[]{:S(2)}) collective-permute-start(bf16[256,1024]{1,0:T(8,128)(2,1)} %param.5), channel_id=1, source_target_pairs={{0,256},{1,257},{2,258},{3,259},{4,260},{5,261},{6,262},{7,263},{8... | collective-permute-start | bytes 1572872 | tf_op jit(solution)/shard_map/ppermute | solution.py:49
  30.9 24.9 %collective-permute-start.3 = (bf16[256,1024]{1,0:T(8,128)(2,1)}, bf16[256,1024]{1,0:T(8,128)(2,1)S(1)}, u32[]{:S(2)}, u32[]{:S(2)}) collective-permute-start(bf16[256,1024]{1,0:T(8,128)(2,1)} %param.5), channel_id=1, source_target_pairs={{0,128},{1,129},{2,130},{3,131},{4,132},{5,133},{6,134},{7,135},{8... | collective-permute-start | bytes 1572872 | tf_op jit(solution)/shard_map/ppermute | solution.py:49
  34.6 23.1 %collective-permute-start.7 = (bf16[256,1024]{1,0:T(8,128)(2,1)}, bf16[256,1024]{1,0:T(8,128)(2,1)S(1)}, u32[]{:S(2)}, u32[]{:S(2)}) collective-permute-start(bf16[256,1024]{1,0:T(8,128)(2,1)} %param.5), channel_id=1, source_target_pairs={{0,384},{1,385},{2,386},{3,387},{4,388},{5,389},{6,390},{7,391},{8... | collective-permute-start | bytes 1572872 | tf_op jit(solution)/shard_map/ppermute | solution.py:49
  38.0 24.2 %collective-permute-start.2 = (bf16[256,1024]{1,0:T(8,128)(2,1)}, bf16[256,1024]{1,0:T(8,128)(2,1)}, u32[]{:S(2)}, u32[]{:S(2)}) collective-permute-start(bf16[256,1024]{1,0:T(8,128)(2,1)} %param.5), channel_id=1, source_target_pairs={{0,1},{1,0},{2,3},{3,2},{4,5},{5,4},{6,7},{7,6},{8,9},{9,8},{10,11... | collective-permute-start | bytes 1572872 | tf_op jit(solution)/shard_map/ppermute | solution.py:114
  47.6 16.3 %collective-permute-start.6 = (bf16[256,1024]{1,0:T(8,128)(2,1)}, bf16[256,1024]{1,0:T(8,128)(2,1)}, u32[]{:S(2)}, u32[]{:S(2)}) collective-permute-start(bf16[256,1024]{1,0:T(8,128)(2,1)} %collective-permute-done.5), channel_id=1, source_target_pairs={{0,1},{1,0},{2,3},{3,2},{4,5},{5,4},{6,7},{7,6},{8,9},{9,8},{10,11... | collective-permute-start | bytes 1572872 | tf_op jit(solution)/shard_map/ppermute | solution.py:114
  55.8 9.5 %collective-permute-start.4 = (bf16[256,1024]{1,0:T(8,128)(2,1)S(1)}, bf16[256,1024]{1,0:T(8,128)(2,1)S(1)}, u32[]{:S(2)}, u32[]{:S(2)}) collective-permute-start(bf16[256,1024]{1,0:T(8,128)(2,1)S(1)} %collective-permute-done.3), channel_id=1, source_target_pairs={{0,1},{1,0},{2,3},{3,2},{4,5},{5,4},{6,7},{7,6},{8,9},{9,8},{10,11... | collective-permute-start | bytes 1572872 | tf_op jit(solution)/shard_map/ppermute | solution.py:114
  57.7 6.2 %copy-start.3 = (bf16[256,1024]{1,0:T(8,128)(2,1)}, bf16[256,1024]{1,0:T(8,128)(2,1)S(1)}, u32[]{:S(2)}) copy-start(bf16[256,1024]{1,0:T(8,128)(2,1)S(1)} %collective-permute-done.7) | copy-start | bytes 1572868
  57.7 7.9 %collective-permute-start.8 = (bf16[256,1024]{1,0:T(8,128)(2,1)S(1)}, bf16[256,1024]{1,0:T(8,128)(2,1)}, u32[]{:S(2)}, u32[]{:S(2)}) collective-permute-start(bf16[256,1024]{1,0:T(8,128)(2,1)S(1)} %collective-permute-done.7), channel_id=1, source_target_pairs={{0,1},{1,0},{2,3},{3,2},{4,5},{5,4},{6,7},{7,6},{8,9},{9,8},{10,11... | collective-permute-start | bytes 1572872 | tf_op jit(solution)/shard_map/ppermute | solution.py:114
  67.0 14.6 %copy-start.6 = (bf16[256,1024]{1,0:T(8,128)(2,1)S(1)}, bf16[256,1024]{1,0:T(8,128)(2,1)}, u32[]{:S(2)}) copy-start(bf16[256,1024]{1,0:T(8,128)(2,1)} %param.9) | copy-start | bytes 1572868
  67.9 31.7 %collective-permute-start.10 = (f32[256,128]{0,1:T(8,128)}, f32[256,128]{0,1:T(8,128)S(1)}, u32[]{:S(2)}, u32[]{:S(2)}) collective-permute-start(f32[256,128]{0,1:T(8,128)} %get-tuple-element.12), channel_id=1, source_target_pairs={{0,128},{1,129},{2,256},{3,257},{4,384},{5,385},{6,0},{7,1},{8,136... | collective-permute-start | bytes 393224 | tf_op jit(solution)/shard_map/ppermute | solution.py:49
  70.3 29.4 %collective-permute-start.11 = (f32[256,128]{0,1:T(8,128)S(1)}, f32[256,128]{0,1:T(8,128)S(1)}, u32[]{:S(2)}, u32[]{:S(2)}) collective-permute-start(f32[256,128]{0,1:T(8,128)S(1)} %get-tuple-element.13), channel_id=1, source_target_pairs={{0,256},{1,257},{2,384},{3,385},{4,0},{5,1},{6,128},{7,129},{8,264... | collective-permute-start | bytes 393224 | tf_op jit(solution)/shard_map/ppermute | solution.py:49
  73.9 25.7 %collective-permute-start.9 = (f32[256,128]{0,1:T(8,128)S(1)}, f32[256,128]{0,1:T(8,128)S(1)}, u32[]{:S(2)}, u32[]{:S(2)}) collective-permute-start(f32[256,128]{0,1:T(8,128)S(1)} %get-tuple-element.14), channel_id=1, source_target_pairs={{0,0},{1,1},{2,128},{3,129},{4,256},{5,257},{6,384},{7,385},{8,8},... | collective-permute-start | bytes 393224 | tf_op jit(solution)/shard_map/ppermute | solution.py:49
  78.1 21.6 %collective-permute-start.12 = (f32[256,128]{0,1:T(8,128)S(1)}, f32[256,128]{0,1:T(8,128)S(1)}, u32[]{:S(2)}, u32[]{:S(2)}) collective-permute-start(f32[256,128]{0,1:T(8,128)S(1)} %get-tuple-element.15), channel_id=1, source_target_pairs={{0,384},{1,385},{2,0},{3,1},{4,128},{5,129},{6,256},{7,257},{8,392... | collective-permute-start | bytes 393224 | tf_op jit(solution)/shard_map/ppermute | solution.py:49
  102.0 1.9 %copy-start.7 = (bf16[256,128]{1,0:T(8,128)(2,1)S(1)}, bf16[256,128]{1,0:T(8,128)(2,1)}, u32[]{:S(2)}) copy-start(bf16[256,128]{1,0:T(8,128)(2,1)} %param.8) | copy-start | bytes 196612
  102.0 2.3 %copy-start.1 = (f32[8,256,256]{1,2,0:T(8,128)S(1)}, f32[8,256,256]{1,2,0:T(8,128)}, u32[]{:S(2)}) copy-start(f32[8,256,256]{1,2,0:T(8,128)} %get-tuple-element.19) | copy-start | bytes 6291460
  104.8 1.0 copy-start.5
  106.2 23.9 %collective-permute-start.16 = (bf16[256,128]{1,0:T(8,128)(2,1)S(1)}, bf16[256,128]{1,0:T(8,128)(2,1)S(1)}, u32[]{:S(2)}, u32[]{:S(2)}) collective-permute-start(bf16[256,128]{1,0:T(8,128)(2,1)S(1)} %fusion.21), channel_id=1, source_target_pairs={{384,0},{385,1},{0,2},{1,3},{128,4},{129,5},{256,6},{257,7},{392,8... | collective-permute-start | bytes 196616 | tf_op jit(solution)/shard_map/ppermute | solution.py:49
  113.3 16.9 %collective-permute-start.15 = (bf16[256,128]{1,0:T(8,128)(2,1)S(1)}, bf16[256,128]{1,0:T(8,128)(2,1)S(1)}, u32[]{:S(2)}, u32[]{:S(2)}) collective-permute-start(bf16[256,128]{1,0:T(8,128)(2,1)S(1)} %fusion.21), channel_id=1, source_target_pairs={{256,0},{257,1},{384,2},{385,3},{0,4},{1,5},{128,6},{129,7},{264,8... | collective-permute-start | bytes 196616 | tf_op jit(solution)/shard_map/ppermute | solution.py:49
  118.9 11.2 %collective-permute-start.14 = (bf16[256,128]{1,0:T(8,128)(2,1)S(1)}, bf16[256,128]{1,0:T(8,128)(2,1)S(1)}, u32[]{:S(2)}, u32[]{:S(2)}) collective-permute-start(bf16[256,128]{1,0:T(8,128)(2,1)S(1)} %fusion.21), channel_id=1, source_target_pairs={{128,0},{129,1},{256,2},{257,3},{384,4},{385,5},{0,6},{1,7},{136,8... | collective-permute-start | bytes 196616 | tf_op jit(solution)/shard_map/ppermute | solution.py:49
  120.9 11.8 %collective-permute-start.13 = (bf16[256,128]{1,0:T(8,128)(2,1)S(1)}, bf16[256,128]{1,0:T(8,128)(2,1)S(1)}, u32[]{:S(2)}, u32[]{:S(2)}) collective-permute-start(bf16[256,128]{1,0:T(8,128)(2,1)S(1)} %fusion.21), channel_id=1, source_target_pairs={{0,0},{1,1},{128,2},{129,3},{256,4},{257,5},{384,6},{385,7},{8,8},... | collective-permute-start | bytes 196616 | tf_op jit(solution)/shard_map/ppermute | solution.py:49
  134.4 4.1 %copy-start.4 = (bf16[256,1024]{1,0:T(8,128)(2,1)S(1)}, bf16[256,1024]{1,0:T(8,128)(2,1)}, u32[]{:S(2)}) copy-start(bf16[256,1024]{1,0:T(8,128)(2,1)} %copy-done.3) | copy-start | bytes 1572868
  143.5 22.6 %all-to-all-start.1 = ((bf16[8,256,128]{1,2,0:T(8,128)(2,1)}), bf16[8,256,128]{1,2,0:T(8,128)(2,1)S(1)}, u32[]{:S(2)}, u32[]{:S(2)}) async-start(bf16[8,256,128]{1,2,0:T(8,128)(2,1)} %copy.41), calls=%async_computation.1 | async-start | bytes 1048576 | tf_op jit(solution)/shard_map/all_to_all | solution.py:139
  166.6 11.4 %collective-permute-start.18 = (bf16[128,128]{1,0:T(8,128)(2,1)S(1)}, bf16[128,128]{1,0:T(8,128)(2,1)S(1)}, u32[]{:S(2)}, u32[]{:S(2)}) collective-permute-start(bf16[128,128]{1,0:T(8,128)(2,1)S(1)} %bitcast.162), channel_id=1, source_target_pairs={{0,8},{1,9},{2,136},{3,137},{4,264},{5,265},{6,392},{7,393},{8,0},... | collective-permute-start | bytes 98312 | tf_op jit(solution)/shard_map/ppermute | solution.py:49
  171.7 9.1 %collective-permute-start.17 = (bf16[128,128]{1,0:T(8,128)(2,1)S(1)}, bf16[128,128]{1,0:T(8,128)(2,1)S(1)}, u32[]{:S(2)}, u32[]{:S(2)}) collective-permute-start(bf16[128,128]{1,0:T(8,128)(2,1)S(1)} %bitcast.161), channel_id=1, source_target_pairs={{0,0},{1,1},{2,128},{3,129},{4,256},{5,257},{6,384},{7,385},{8,8},... | collective-permute-start | bytes 98312 | tf_op jit(solution)/shard_map/ppermute | solution.py:49

commit v3 on v0

--- a/solution.py
+++ b/solution.py
@@ -3,19 +3,73 @@
 from jax import lax
 from jax.sharding import PartitionSpec as P
 
+X, Y, ZH, U, V, C = 4, 8, 2, 2, 2, 2
+HALF = Y // 2
+BOTH = ("dp", "head")
 
-def on_device(tokens, key_weight, queries, values, out_grad):
+
+def dp_of(x, y, zh):
+    return (x * Y + y) * ZH + zh
+
+
+def place(x, y, zh, u, v, c):
+    return dp_of(x, y, zh) * U * V * C + (u * V + v) * C + c
+
+
+DEVICES = [
+    (x, y, zh, u, v, c)
+    for x in range(X)
+    for y in range(Y)
+    for zh in range(ZH)
+    for u in range(U)
+    for v in range(V)
+    for c in range(C)
+]
+ALONG_Y = [[dp_of(x, y, zh) for y in range(Y)] for x in range(X) for zh in range(ZH)]
+ALONG_XV = [
+    [place(x, y, zh, u, v, c) for x in range(X) for v in range(V)]
+    for y in range(Y)
+    for zh in range(ZH)
+    for u in range(U)
+    for c in range(C)
+]
+CORES = [(h, h ^ 1) for h in range(U * V * C)]
+
+
+def to_features(j):
+    return [
+        (place(x, y, zh, u, v, c), place(u * V + v, y, zh, (x % 2) ^ j, c, x // 2))
+        for x, y, zh, u, v, c in DEVICES
+    ]
+
+
+def to_owner(flip):
+    return [
+        (place(x, y, zh, u, v, c), place(x, v * HALF + y % HALF, zh ^ flip, u, y // HALF, c))
+        for x, y, zh, u, v, c in DEVICES
+    ]
+
+
+def spread(block, axis, groups):
+    n = len(groups[0])
+    many = jnp.broadcast_to(block[None], (n,) + block.shape)
+    return lax.all_to_all(many, axis, 0, 0, tiled=True, axis_index_groups=groups)
+
+
+def in_order(own, other, position):
+    return jnp.where(position == 0, jnp.stack([own, other]), jnp.stack([other, own]))
+
+
+def sequences(parts, first):
+    low = [jnp.where(first % 2 == 0, parts[i], parts[i ^ 1]) for i in range(X)]
+    return [jnp.where(first // 2 == 0, low[i], low[i ^ 2]) for i in range(X)]
+
+
+def attention(queries, keys, values, out_grad):
     width = values.shape[1]
-    length = tokens.shape[0]
+    length = queries.shape[0]
     group = queries.shape[1] // width
     scale = width ** (-0.5)
-    gathered = lax.all_gather(tokens, "head", axis=1, tiled=True)
-    columns = gathered
-    keys = jnp.dot(
-        columns,
-        lax.all_gather(key_weight, "dp", axis=0, tiled=True),
-        preferred_element_type=jnp.float32,
-    ).astype(jnp.bfloat16)
     query_heads = queries.reshape(length, group, width)
     grad_heads = out_grad.reshape(length, group, width)
     scores = (
@@ -46,22 +100,61 @@
     value_grad = jnp.einsum(
         "gqk,qgd->kd", weights, grad_heads, preferred_element_type=jnp.float32
     ).astype(jnp.bfloat16)
-    columns = gathered
-    weight_grad = lax.psum_scatter(
-        lax.dot_general(
-            columns, key_grad, (((0,), (0,)), ((), ())), preferred_element_type=jnp.float32
-        ),
-        "dp",
-        scatter_dimension=0,
-        tiled=True,
+    return query_grad.reshape(length, group * width), key_grad, value_grad
+
+
+def step(tokens, key_weight, queries, values, out_grad):
+    f32, bf16 = jnp.float32, jnp.bfloat16
+    length, feats = tokens.shape
+    rows, width = key_weight.shape
+    dp, head = lax.axis_index("dp"), lax.axis_index("head")
+    zh, u, c = dp % ZH, head // (V * C), head % C
+    first = 2 * c + u
+    weight = []
+    for flip in range(ZH):
+        weight.append(lax.ppermute(key_weight, BOTH, to_owner(flip)))
+    blocks = []
+    for j in range(U):
+        blocks.append(lax.ppermute(tokens, BOTH, to_features(j)))
+    weight = in_order(*weight, zh)
+    weight = spread(weight, "dp", ALONG_Y).reshape(V, feats, width)
+    blocks += [lax.ppermute(block, "head", CORES) for block in blocks]
+    partial = [
+        jnp.stack([jnp.dot(a, weight[v], preferred_element_type=f32) for v in range(V)])
+        for a in blocks
+    ]
+    partial = jnp.stack(sequences(partial, first)).reshape(X * V, length, width)
+    partial = lax.all_to_all(partial, BOTH, 0, 0, tiled=True, axis_index_groups=ALONG_XV)
+    keys = jnp.sum(partial, axis=0).astype(bf16)
+    query_grad, key_grad, value_grad = attention(queries, keys, values, out_grad)
+    grads = spread(key_grad, BOTH, ALONG_XV).reshape(X, V, length, width)
+    grads = sequences([grads[i] for i in range(X)], first)
+    total = jnp.stack(
+        [
+            sum(
+                lax.dot_general(
+                    a, g[v], (((0,), (0,)), ((), ())), preferred_element_type=f32
+                )
+                for a, g in zip(blocks, grads)
+            ).astype(bf16)
+            for v in range(V)
+        ]
     )
-    return (query_grad.reshape(length, group * width), value_grad, weight_grad)
+    total = lax.all_to_all(
+        total.reshape(Y, ZH * rows, width), "dp", 0, 0, tiled=True, axis_index_groups=ALONG_Y
+    )
+    total = jnp.sum(total.astype(f32), axis=0).astype(bf16).reshape(ZH, rows, width)
+    stays = lax.dynamic_index_in_dim(total, zh, 0, keepdims=False)
+    leaves = lax.dynamic_index_in_dim(total, 1 - zh, 0, keepdims=False)
+    weight_grad = lax.ppermute(stays, BOTH, to_owner(0)).astype(f32)
+    weight_grad += lax.ppermute(leaves, BOTH, to_owner(1)).astype(f32)
+    return query_grad, value_grad, weight_grad
 
 
 def solution(mesh):
     placed = (P("dp", "head"), P("dp", "head"), P("dp", "head"), P("dp", "head"), P("dp", "head"))
     return jax.shard_map(
-        on_device,
+        step,
         mesh=mesh,
         in_specs=placed,
         out_specs=(P("dp", "head"), P("dp", "head"), P("dp", "head")),

time: 685 us -> 155 us (0.23)
  the two profiles are of different devices: /device:TPU:64 before, /device:TPU:32 now
where the time goes in v3:
time: 155 us; the launch traced here: 154 us
  starting transfers between devices  72.5 us (47%)
  waiting for transfers between devices  47.2 us (30%)
  blocking collectives  12.8 us (8%)
  matrix products  10.7 us (7%)
  other arithmetic  5.27 us (3%)
  local copies, waits for them, and re-layouts  4.44 us (3%)
    ppermute x2, starting transfers between devices, step(): weight.append(lax.ppermute(key_weight, BOTH, to_owner(flip)))  18.3 us
    all_to_all x1, waiting for transfers between devices, step(): lax.all_to_all(partial, BOTH, 0, 0, tiled=True, axis_index_groups=ALONG_XV)  15.2 us
    all_to_all x1, starting transfers between devices, step(): lax.all_to_all(partial, BOTH, 0, 0, tiled=True, axis_index_groups=ALONG_XV)  15 us
    all_to_all x1, blocking collectives, spread(): lax.all_to_all(many, axis, 0, 0, tiled=True, axis_index_groups=groups)  12.8 us
    ppermute x2, waiting for transfers between devices, step(): blocks.append(lax.ppermute(tokens, BOTH, to_features(j)))  9.85 us
    all_to_all x1, waiting for transfers between devices, step(): lax.all_to_all(total.reshape(Y, ZH * rows, width), 'dp', 0, 0, tiled=True...  9.84 us
    ppermute x1, waiting for transfers between devices, step(): weight_grad += lax.ppermute(leaves, BOTH, to_owner(1)).astype(f32)  9.14 us
    ppermute x2, starting transfers between devices, step(): blocks += [lax.ppermute(block, 'head', CORES) for block in blocks]  8.71 us
  transfers between devices with their start and end apart: 11, of which 5 were waited for; matrix products, arithmetic and copies ran while one was open for 4% of the time, Pallas kernels for 0%

profile of v3, /device:TPU:32, one launch (start us, length us, event | category | flops | bytes accessed | tf_op | source)
XLA Modules:
  0.0 154.0 jit_solution(890036698112435529)
XLA Ops:
  0.6 10.6 %collective-permute-start.1 = (bf16[128,128]{1,0:T(8,128)(2,1)}, bf16[128,128]{1,0:T(8,128)(2,1)S(1)}, u32[]{:S(2)}, u32[]{:S(2)}) collective-permute-start(bf16[128,128]{1,0:T(8,128)(2,1)} %param.6), channel_id=1, source_target_pairs={{0,8},{1,9},{2,72},{3,73},{4,12},{5,13},{6,76},{7,77},{8,0},{9,1},... | collective-permute-start | bytes 98312 | tf_op jit(solution)/shard_map/ppermute | solution.py:115
  11.3 7.7 %collective-permute-start = (bf16[128,128]{1,0:T(8,128)(2,1)}, bf16[128,128]{1,0:T(8,128)(2,1)S(1)}, u32[]{:S(2)}, u32[]{:S(2)}) collective-permute-start(bf16[128,128]{1,0:T(8,128)(2,1)} %param.6), channel_id=1, source_target_pairs={{0,0},{1,1},{2,64},{3,65},{4,4},{5,5},{6,68},{7,69},{8,8},{9,9},{1... | collective-permute-start | bytes 98312 | tf_op jit(solution)/shard_map/ppermute | solution.py:115
  19.0 3.1 %collective-permute-done = bf16[128,128]{1,0:T(8,128)(2,1)S(1)} collective-permute-done((bf16[128,128]{1,0:T(8,128)(2,1)}, bf16[128,128]{1,0:T(8,128)(2,1)S(1)}, u32[]{:S(2)}, u32[]{:S(2)}) %collective-permute-start) | collective-permute-done | bytes 32800 | tf_op jit(solution)/shard_map/ppermute | solution.py:115
  22.1 0.9 broadcast_in_dim.29
  23.0 7.5 %all-to-all-start = ((bf16[8,2,128,128]{3,2,1,0:T(8,128)(2,1)}), bf16[8,2,128,128]{3,2,1,0:T(8,128)(2,1)S(1)}, u32[]{:S(2)}, u32[]{:S(2)}) async-start(bf16[8,2,128,128]{3,2,1,0:T(8,128)(2,1)} %broadcast_in_dim.29), calls=%async_computation | async-start | bytes 1048576 | tf_op jit(solution)/shard_map/all_to_all | solution.py:56
  30.5 4.3 %collective-permute-start.3 = (bf16[256,1024]{1,0:T(8,128)(2,1)}, bf16[256,1024]{1,0:T(8,128)(2,1)S(1)}, u32[]{:S(2)}, u32[]{:S(2)}) collective-permute-start(bf16[256,1024]{1,0:T(8,128)(2,1)} %param.5), channel_id=1, source_target_pairs={{0,4},{1,6},{2,132},{3,134},{4,260},{5,262},{6,388},{7,390},{8,12}... | collective-permute-start | bytes 1572872 | tf_op jit(solution)/shard_map/ppermute | solution.py:118
  34.8 1.7 %collective-permute-start.2 = (bf16[256,1024]{1,0:T(8,128)(2,1)}, bf16[256,1024]{1,0:T(8,128)(2,1)S(1)}, u32[]{:S(2)}, u32[]{:S(2)}) collective-permute-start(bf16[256,1024]{1,0:T(8,128)(2,1)} %param.5), channel_id=1, source_target_pairs={{0,0},{1,2},{2,128},{3,130},{4,256},{5,258},{6,384},{7,386},{8,8},... | collective-permute-start | bytes 1572872 | tf_op jit(solution)/shard_map/ppermute | solution.py:118
  36.5 9.8 %collective-permute-done.3 = bf16[256,1024]{1,0:T(8,128)(2,1)S(1)} collective-permute-done((bf16[256,1024]{1,0:T(8,128)(2,1)}, bf16[256,1024]{1,0:T(8,128)(2,1)S(1)}, u32[]{:S(2)}, u32[]{:S(2)}) %collective-permute-start.3) | collective-permute-done | bytes 524320 | tf_op jit(solution)/shard_map/ppermute | solution.py:118
  46.4 3.1 %collective-permute-start.5 = (bf16[256,1024]{1,0:T(8,128)(2,1)S(1)}, bf16[256,1024]{1,0:T(8,128)(2,1)S(1)}, u32[]{:S(2)}, u32[]{:S(2)}) collective-permute-start(bf16[256,1024]{1,0:T(8,128)(2,1)S(1)} %collective-permute-done.3), channel_id=1, source_target_pairs={{0,1},{1,0},{2,3},{3,2},{4,5},{5,4},{6,7},{7,6},{8,9},{9,8},{10,11... | collective-permute-start | bytes 1572872 | tf_op jit(solution)/shard_map/ppermute | solution.py:121
  49.5 5.6 %collective-permute-start.4 = (bf16[256,1024]{1,0:T(8,128)(2,1)S(1)}, bf16[256,1024]{1,0:T(8,128)(2,1)S(1)}, u32[]{:S(2)}, u32[]{:S(2)}) collective-permute-start(bf16[256,1024]{1,0:T(8,128)(2,1)S(1)} %collective-permute-done.2), channel_id=1, source_target_pairs={{0,1},{1,0},{2,3},{3,2},{4,5},{5,4},{6,7},{7,6},{8,9},{9,8},{10,11... | collective-permute-start | bytes 1572872 | tf_op jit(solution)/shard_map/ppermute | solution.py:121
  55.5 0.3 convolution_bitcast_fusion.6
  58.0 1.1 pad_maximum_fusion
  59.1 15.0 %all-to-all-start.1 = ((f32[8,256,128]{1,2,0:T(8,128)}), f32[8,256,128]{1,2,0:T(8,128)}, u32[]{:S(2)}, u32[]{:S(2)}) async-start(f32[8,256,128]{1,2,0:T(8,128)} %bitcast.187), calls=%async_computation.1 | async-start | bytes 2097152 | tf_op jit(solution)/shard_map/all_to_all | solution.py:127
  74.1 1.2 copy.20
  75.4 15.2 %all-to-all-done.1 = f32[8,256,128]{1,2,0:T(8,128)} async-done(((f32[8,256,128]{1,2,0:T(8,128)}), f32[8,256,128]{1,2,0:T(8,128)}, u32[]{:S(2)}, u32[]{:S(2)}) %all-to-all-start.1) | async-done | bytes 1048608 | tf_op jit(solution)/shard_map/all_to_all | solution.py:127
  90.6 1.3 reduce_sum.39
  91.9 2.3 %fusion.56 = (f32[8,256]{1,0:T(8,128)S(1)}, f32[8,256,256]{1,2,0:T(8,128)}) fusion(pred[256,256]{0,1:T(8,128)(4,1)S(1)} %iota_compare_fusion, bf16[256,128]{0,1:T(8,128)(2,1)S(1)} %reduce_sum.39, bf16[256,1024]{1,0:T(8,128)(2,1)S(1)} %copy-done), kind=kOutput, calls=%fused_computation.97 | convolution fusion | flops 136839424 | bytes 2760704 | tf_op jit(solution)/shard_map/sub | solution.py:83
  94.2 1.9 %fusion.21 = bf16[8,256,256]{1,2,0:T(8,128)(2,1)S(1)} fusion(f32[8,256,256]{1,2,0:T(8,128)} %get-tuple-element.22, f32[8,256]{1,0:T(8,128)S(1)} %get-tuple-element.21), kind=kLoop, calls=%fused_computation.42 | loop fusion | flops 1048576 | bytes 3153920 | tf_op jit(solution)/shard_map/convert_element_type | solution.py:85
  96.2 0.4 fusion.8
  96.6 0.4 fusion.2
  97.1 0.4 fusion.17
  97.6 12.8 %all_to_all.20 = bf16[8,256,128]{2,1,0:T(8,128)(2,1)S(1)} all-to-all(bf16[8,256,128]{2,1,0:T(8,128)(2,1)S(1)} %broadcast_in_dim.33), channel_id=1, replica_groups={{0,2,128,130,256,258,384,386},{1,3,129,131,257,259,385,387},{4,6,132,13..., dimensions={0} | all-to-all | bytes 1048576 | tf_op jit(solution)/shard_map/all_to_all | solution.py:56
  112.7 1.0 copy.27
  113.7 7.2 %all-to-all-start.3 = ((bf16[8,256,128]{2,1,0:T(8,128)(2,1)}), bf16[8,256,128]{2,1,0:T(8,128)(2,1)S(1)}, u32[]{:S(2)}, u32[]{:S(2)}) async-start(bf16[8,256,128]{2,1,0:T(8,128)(2,1)} %bitcast.46), calls=%async_computation.3 | async-start | bytes 1048576 | tf_op jit(solution)/shard_map/all_to_all | solution.py:143
  120.9 1.1 fusion.16
  122.0 9.8 %all-to-all-done.3 = bf16[8,256,128]{2,1,0:T(8,128)(2,1)S(1)} async-done(((bf16[8,256,128]{2,1,0:T(8,128)(2,1)}), bf16[8,256,128]{2,1,0:T(8,128)(2,1)S(1)}, u32[]{:S(2)}, u32[]{:S(2)}) %all-to-all-start.3) | async-done | bytes 524320 | tf_op jit(solution)/shard_map/all_to_all | solution.py:143
  131.9 7.8 %collective-permute-start.6 = (bf16[128,128]{1,0:T(8,128)(2,1)S(1)}, bf16[128,128]{1,0:T(8,128)(2,1)S(1)}, u32[]{:S(2)}, u32[]{:S(2)}) collective-permute-start(bf16[128,128]{1,0:T(8,128)(2,1)S(1)} %get-tuple-element.19), channel_id=1, source_target_pairs={{0,0},{1,1},{2,64},{3,65},{4,4},{5,5},{6,68},{7,69},{8,8},{9,9},{1... | collective-permute-start | bytes 98312 | tf_op jit(solution)/shard_map/ppermute | solution.py:149
  139.7 1.9 %collective-permute-start.7 = (bf16[128,128]{1,0:T(8,128)(2,1)S(1)}, bf16[128,128]{1,0:T(8,128)(2,1)S(1)}, u32[]{:S(2)}, u32[]{:S(2)}) collective-permute-start(bf16[128,128]{1,0:T(8,128)(2,1)S(1)} %get-tuple-element.20), channel_id=1, source_target_pairs={{0,8},{1,9},{2,72},{3,73},{4,12},{5,13},{6,76},{7,77},{8,0},{9,1},... | collective-permute-start | bytes 98312 | tf_op jit(solution)/shard_map/ppermute | solution.py:150
  141.7 1.5 fusion.7
  143.2 1.0 copy.28
  144.2 9.1 %collective-permute-done.7 = bf16[128,128]{1,0:T(8,128)(2,1)S(1)} collective-permute-done((bf16[128,128]{1,0:T(8,128)(2,1)S(1)}, bf16[128,128]{1,0:T(8,128)(2,1)S(1)}, u32[]{:S(2)}, u32[]{:S(2)}) %collective-permute-start.7) | collective-permute-done | bytes 32800 | tf_op jit(solution)/shard_map/ppermute | solution.py:150
  153.4 0.6 convert_add_fusion
  (43 shorter events, 4.9 us)
Async XLA Ops:
  0.6 91.3 %copy-start = (bf16[256,1024]{1,0:T(8,128)(2,1)S(1)}, bf16[256,1024]{1,0:T(8,128)(2,1)}, u32[]{:S(2)}) copy-start(bf16[256,1024]{1,0:T(8,128)(2,1)} %param.7) | copy-start | bytes 1572868
  0.6 18.4 %collective-permute-start.1 = (bf16[128,128]{1,0:T(8,128)(2,1)}, bf16[128,128]{1,0:T(8,128)(2,1)S(1)}, u32[]{:S(2)}, u32[]{:S(2)}) collective-permute-start(bf16[128,128]{1,0:T(8,128)(2,1)} %param.6), channel_id=1, source_target_pairs={{0,8},{1,9},{2,72},{3,73},{4,12},{5,13},{6,76},{7,77},{8,0},{9,1},... | collective-permute-start | bytes 98312 | tf_op jit(solution)/shard_map/ppermute | solution.py:115
  11.3 10.8 %collective-permute-start = (bf16[128,128]{1,0:T(8,128)(2,1)}, bf16[128,128]{1,0:T(8,128)(2,1)S(1)}, u32[]{:S(2)}, u32[]{:S(2)}) collective-permute-start(bf16[128,128]{1,0:T(8,128)(2,1)} %param.6), channel_id=1, source_target_pairs={{0,0},{1,1},{2,64},{3,65},{4,4},{5,5},{6,68},{7,69},{8,8},{9,9},{1... | collective-permute-start | bytes 98312 | tf_op jit(solution)/shard_map/ppermute | solution.py:115
  23.0 32.1 %all-to-all-start = ((bf16[8,2,128,128]{3,2,1,0:T(8,128)(2,1)}), bf16[8,2,128,128]{3,2,1,0:T(8,128)(2,1)S(1)}, u32[]{:S(2)}, u32[]{:S(2)}) async-start(bf16[8,2,128,128]{3,2,1,0:T(8,128)(2,1)} %broadcast_in_dim.29), calls=%async_computation | async-start | bytes 1048576 | tf_op jit(solution)/shard_map/all_to_all | solution.py:56
  30.5 15.8 %collective-permute-start.3 = (bf16[256,1024]{1,0:T(8,128)(2,1)}, bf16[256,1024]{1,0:T(8,128)(2,1)S(1)}, u32[]{:S(2)}, u32[]{:S(2)}) collective-permute-start(bf16[256,1024]{1,0:T(8,128)(2,1)} %param.5), channel_id=1, source_target_pairs={{0,4},{1,6},{2,132},{3,134},{4,260},{5,262},{6,388},{7,390},{8,12}... | collective-permute-start | bytes 1572872 | tf_op jit(solution)/shard_map/ppermute | solution.py:118
  34.8 14.7 %collective-permute-start.2 = (bf16[256,1024]{1,0:T(8,128)(2,1)}, bf16[256,1024]{1,0:T(8,128)(2,1)S(1)}, u32[]{:S(2)}, u32[]{:S(2)}) collective-permute-start(bf16[256,1024]{1,0:T(8,128)(2,1)} %param.5), channel_id=1, source_target_pairs={{0,0},{1,2},{2,128},{3,130},{4,256},{5,258},{6,384},{7,386},{8,8},... | collective-permute-start | bytes 1572872 | tf_op jit(solution)/shard_map/ppermute | solution.py:118
  46.4 10.1 %collective-permute-start.5 = (bf16[256,1024]{1,0:T(8,128)(2,1)S(1)}, bf16[256,1024]{1,0:T(8,128)(2,1)S(1)}, u32[]{:S(2)}, u32[]{:S(2)}) collective-permute-start(bf16[256,1024]{1,0:T(8,128)(2,1)S(1)} %collective-permute-done.3), channel_id=1, source_target_pairs={{0,1},{1,0},{2,3},{3,2},{4,5},{5,4},{6,7},{7,6},{8,9},{9,8},{10,11... | collective-permute-start | bytes 1572872 | tf_op jit(solution)/shard_map/ppermute | solution.py:121
  49.5 7.6 %collective-permute-start.4 = (bf16[256,1024]{1,0:T(8,128)(2,1)S(1)}, bf16[256,1024]{1,0:T(8,128)(2,1)S(1)}, u32[]{:S(2)}, u32[]{:S(2)}) collective-permute-start(bf16[256,1024]{1,0:T(8,128)(2,1)S(1)} %collective-permute-done.2), channel_id=1, source_target_pairs={{0,1},{1,0},{2,3},{3,2},{4,5},{5,4},{6,7},{7,6},{8,9},{9,8},{10,11... | collective-permute-start | bytes 1572872 | tf_op jit(solution)/shard_map/ppermute | solution.py:121
  59.1 31.5 %all-to-all-start.1 = ((f32[8,256,128]{1,2,0:T(8,128)}), f32[8,256,128]{1,2,0:T(8,128)}, u32[]{:S(2)}, u32[]{:S(2)}) async-start(f32[8,256,128]{1,2,0:T(8,128)} %bitcast.187), calls=%async_computation.1 | async-start | bytes 2097152 | tf_op jit(solution)/shard_map/all_to_all | solution.py:127
  94.2 1.9 %copy-start.5 = (bf16[256,128]{1,0:T(8,128)(2,1)S(1)}, bf16[256,128]{1,0:T(8,128)(2,1)}, u32[]{:S(2)}) copy-start(bf16[256,128]{1,0:T(8,128)(2,1)} %param.8) | copy-start | bytes 196612
  94.2 2.3 %copy-start.3 = (f32[8,256,256]{1,2,0:T(8,128)S(1)}, f32[8,256,256]{1,2,0:T(8,128)}, u32[]{:S(2)}) copy-start(f32[8,256,256]{1,2,0:T(8,128)} %get-tuple-element.22) | copy-start | bytes 6291460
  96.2 1.0 copy-start.1
  97.1 13.4 %copy-start.4 = (bf16[8,256,256]{1,2,0:T(8,128)(2,1)}, bf16[8,256,256]{1,2,0:T(8,128)(2,1)S(1)}, u32[]{:S(2)}) copy-start(bf16[8,256,256]{1,2,0:T(8,128)(2,1)S(1)} %fusion.2) | copy-start | bytes 3145732
  112.4 8.5 %copy-start.2 = (bf16[8,256,256]{1,2,0:T(8,128)(2,1)S(1)}, bf16[8,256,256]{1,2,0:T(8,128)(2,1)}, u32[]{:S(2)}) copy-start(bf16[8,256,256]{1,2,0:T(8,128)(2,1)} %copy-done.1) | copy-start | bytes 3145732
  113.7 18.1 %all-to-all-start.3 = ((bf16[8,256,128]{2,1,0:T(8,128)(2,1)}), bf16[8,256,128]{2,1,0:T(8,128)(2,1)S(1)}, u32[]{:S(2)}, u32[]{:S(2)}) async-start(bf16[8,256,128]{2,1,0:T(8,128)(2,1)} %bitcast.46), calls=%async_computation.3 | async-start | bytes 1048576 | tf_op jit(solution)/shard_map/all_to_all | solution.py:143
  131.9 12.3 %collective-permute-start.6 = (bf16[128,128]{1,0:T(8,128)(2,1)S(1)}, bf16[128,128]{1,0:T(8,128)(2,1)S(1)}, u32[]{:S(2)}, u32[]{:S(2)}) collective-permute-start(bf16[128,128]{1,0:T(8,128)(2,1)S(1)} %get-tuple-element.19), channel_id=1, source_target_pairs={{0,0},{1,1},{2,64},{3,65},{4,4},{5,5},{6,68},{7,69},{8,8},{9,9},{1... | collective-permute-start | bytes 98312 | tf_op jit(solution)/shard_map/ppermute | solution.py:149
  139.7 13.6 %collective-permute-start.7 = (bf16[128,128]{1,0:T(8,128)(2,1)S(1)}, bf16[128,128]{1,0:T(8,128)(2,1)S(1)}, u32[]{:S(2)}, u32[]{:S(2)}) collective-permute-start(bf16[128,128]{1,0:T(8,128)(2,1)S(1)} %get-tuple-element.20), channel_id=1, source_target_pairs={{0,8},{1,9},{2,72},{3,73},{4,12},{5,13},{6,76},{7,77},{8,0},{9,1},... | collective-permute-start | bytes 98312 | tf_op jit(solution)/shard_map/ppermute | solution.py:150
